TPU v7x, 128 devices: a whole 4x4x4 slice. The times are simulated.
128 devices in a mesh: tx: 16 (over x, y), ty: 8 (over z, core).
Axes of the slice: x: 4, y: 4, z: 4, core: 2. Of those that a mesh axis runs over, the one named last changes fastest.
Arguments:
- mag: float32 [3, 2048, 2048], P(None, 'tx', 'ty'), may hold values from -1 to 1, as said below
- occupancy: int32 [2048, 2048], P('tx', 'ty'), may hold values from 0 to 1
- kernel_spectrum: float32 [4, 4096, 4096], P(None, ('tx', 'ty')), may hold values from -0.5 to 1, as said below
Outputs:
- mag_next: float32 [3, 2048, 2048], P(None, 'tx', 'ty')
- mean_rate: float32 [3, 2048, 2048], P(None, 'tx', 'ty')
Inputs may be any that keep to these rules, and one draw needn't show every extreme that they name: `mag`: each cell's three components have unit length. `kernel_spectrum`: each component is unchanged under (y frequency, x frequency) -> ((4096 - y frequency) mod 2 * 2048, (4096 - x frequency) mod 2 * 2048).
All inputs are finite; a program needn't handle non-finite values.
Results may differ from a plain program's by a relative error of at most 0.00005.
Values sent between devices are 32-bit elements; how exact they have to be, the bound alone decides.
A program may use at most 192 MiB of HBM per device.

v0:
```python
import math

import jax
import jax.numpy as jnp
from jax import lax
from jax.sharding import Mesh
from jax.sharding import PartitionSpec as P

TX_TY = ("tx", "ty_0", "ty_1")
TY = ("ty_0", "ty_1")


DAMPING = 0.3
STIFFNESS = 0.25
TIME_STEP = 0.25


def split_up(array, dim, length):
    shape = array.shape
    tiles = array.reshape(*shape[:dim], length, shape[dim] // length, *shape[dim + 1 :])
    return jnp.moveaxis(tiles, dim, 0)


def joined_along(tiles, dim):
    shape = list(tiles.shape[1:])
    shape[dim] *= tiles.shape[0]
    return jnp.moveaxis(tiles, 0, dim).reshape(shape)


def moved_by_axis(tiles, axes, turns):
    shape = [lax.axis_size(a) for a in axes]
    tiles = tiles.reshape(*shape, *tiles.shape[1:])
    for k in turns:
        tiles = lax.all_to_all(tiles, axes[k], split_axis=k, concat_axis=k, tiled=True)
    return tiles.reshape(-1, *tiles.shape[len(axes) :])


def two_step_exchange(array, groups, turns, split_dim, concat_dim):
    length = lax.axis_size(groups[0]) * lax.axis_size(groups[1])
    tiles = split_up(array, split_dim, length)
    return joined_along(moved_by_axis(tiles, groups, turns), concat_dim)


def with_halo(array, sides, width):
    edges = {}
    for axis, dim in sides:
        size, length = (lax.axis_size(axis), array.shape[dim])
        up = [(i, (i + 1) % size) for i in range(size - 1)]
        last = lax.slice_in_dim(array, length - width, length, axis=dim)
        initial = lax.slice_in_dim(array, 0, width, axis=dim)
        edges[dim] = (
            lax.ppermute(last, axis, up),
            lax.ppermute(initial, axis, [(b, a) for a, b in up]),
        )
    done = []
    for _, dim in sides:
        low, high = edges[dim]
        around = [(width, width) if d in done else (0, 0) for d in range(array.ndim)]
        array = jnp.concatenate([jnp.pad(low, around), array, jnp.pad(high, around)], axis=dim)
        done.append(dim)
    return array


def contract(form, left, right):
    return jnp.einsum(form, left, right, precision=lax.Precision.HIGHEST)


def trig(first_count, second_count, length):
    first_index = jnp.arange(first_count, dtype=jnp.int32)
    second_index = jnp.arange(second_count, dtype=jnp.int32)
    product = first_index[:, None] * second_index[None, :] % length
    angle = product.astype(jnp.float32) * (2.0 * math.pi / length)
    return (jnp.cos(angle), jnp.sin(angle))


def factors(length):
    bits = length.bit_length() - 1
    outer_len = 1 << bits // 2
    return (length // outer_len, outer_len)


def turn(values):
    paired = values.reshape(values.shape[:-1] + (values.shape[-1] // 2, 2))
    return jnp.stack([-paired[..., 1], paired[..., 0]], axis=-1).reshape(values.shape)


def y_forward(rows):
    comps, row_count, width = rows.shape
    length = 2 * width
    first_len, second_len = factors(length)
    shaped = rows.reshape(comps, row_count, first_len // 2, second_len)
    cos_one, sin_one = trig(first_len // 2, first_len, first_len)
    real_part = contract("mrab,ac->rbcm", shaped, cos_one)
    imag_part = -contract("mrab,ac->rbcm", shaped, sin_one)
    section = jnp.stack([real_part, imag_part], axis=-1).reshape(
        row_count, second_len, first_len, 2 * comps
    )
    twist_cos, twist_sin = trig(second_len, first_len, length)
    section = section * twist_cos[None, :, :, None] - turn(section) * twist_sin[None, :, :, None]
    cos_two, sin_two = trig(second_len, second_len, second_len)
    result = contract("rbcz,bd->rdcz", section, cos_two) - contract(
        "rbcz,bd->rdcz", turn(section), sin_two
    )
    return result.reshape(row_count, length * 2 * comps)


def x_forward(columns):
    half, width = columns.shape
    length = 2 * half
    first_len, second_len = factors(length)
    shaped = columns.reshape(first_len // 2, second_len, width)
    cos_one, sin_one = trig(first_len // 2, first_len, first_len)
    section = contract("abz,ac->cbz", shaped, cos_one) - contract(
        "abz,ac->cbz", turn(shaped), sin_one
    )
    twist_cos, twist_sin = trig(first_len, second_len, length)
    section = section * twist_cos[:, :, None] - turn(section) * twist_sin[:, :, None]
    cos_two, sin_two = trig(second_len, second_len, second_len)
    result = contract("cbz,bd->dcz", section, cos_two) - contract(
        "cbz,bd->dcz", turn(section), sin_two
    )
    return result.reshape(length, width)


def x_inverse(spectra):
    length, width = spectra.shape
    first_len, second_len = factors(length)
    shaped = spectra.reshape(second_len, first_len, width)
    cos_one, sin_one = trig(second_len, second_len, second_len)
    section = contract("dcz,db->bcz", shaped, cos_one) + contract(
        "dcz,db->bcz", turn(shaped), sin_one
    )
    twist_cos, twist_sin = trig(second_len, first_len, length)
    section = section * twist_cos[:, :, None] + turn(section) * twist_sin[:, :, None]
    cos_two, sin_two = trig(first_len, first_len // 2, first_len)
    result = contract("bcz,ca->abz", section, cos_two) + contract(
        "bcz,ca->abz", turn(section), sin_two
    )
    return result.reshape(length // 2, width) * (1.0 / length)


def y_inverse(spectra):
    row_count = spectra.shape[0]
    length = spectra.shape[1] // 6
    first_len, second_len = factors(length)
    shaped = spectra.reshape(row_count, second_len, first_len, 6)
    cos_one, sin_one = trig(second_len, second_len, second_len)
    section = contract("rdcz,db->rbcz", shaped, cos_one) + contract(
        "rdcz,db->rbcz", turn(shaped), sin_one
    )
    twist_cos, twist_sin = trig(second_len, first_len, length)
    section = section * twist_cos[None, :, :, None] + turn(section) * twist_sin[None, :, :, None]
    parts = section.reshape(row_count, second_len, first_len, 3, 2)
    cos_two, sin_two = trig(first_len, first_len // 2, first_len)
    result = contract("rbcm,ca->mrab", parts[..., 0], cos_two) - contract(
        "rbcm,ca->mrab", parts[..., 1], sin_two
    )
    return result.reshape(3, row_count, length // 2) * (1.0 / length)


def cross(left, right):
    return jnp.stack(
        [
            left[1] * right[2] - left[2] * right[1],
            left[2] * right[0] - left[0] * right[2],
            left[0] * right[1] - left[1] * right[0],
        ]
    )


def rim_sum(padded):
    return (
        padded[..., 2:, 1:-1]
        + padded[..., :-2, 1:-1]
        + padded[..., 1:-1, 2:]
        + padded[..., 1:-1, :-2]
    )


def send_out(spectra):
    return lax.all_to_all(spectra, TX_TY, split_axis=1, concat_axis=0, tiled=True)


def send_back(partial_value):
    return lax.all_to_all(partial_value, TX_TY, split_axis=0, concat_axis=1, tiled=True)


def apply_kernel(kernel, spectra):
    length, width = spectra.shape
    split = spectra.reshape(length, width // 6, 3, 2)
    gains = kernel[..., None]
    field_x = -(gains[0] * split[:, :, 0] + gains[3] * split[:, :, 1])
    field_y = -(gains[3] * split[:, :, 0] + gains[1] * split[:, :, 1])
    field_z = -(gains[2] * split[:, :, 2])
    return jnp.stack([field_x, field_y, field_z], axis=2).reshape(length, width)


def demag(field, kernel):
    rows = two_step_exchange(field, ("ty_0", "ty_1"), (1, 0), 1, 2)
    spectra = y_forward(rows)
    columns = send_out(spectra)
    product = apply_kernel(kernel, x_forward(columns))
    partial_value = x_inverse(product)
    returned = send_back(partial_value)
    spatial = y_inverse(returned)
    return two_step_exchange(spatial, ("ty_0", "ty_1"), (0, 1), 2, 1)


def body(mag, occupancy, kernel_spectrum):
    occ = occupancy.astype(jnp.float32)
    start = mag * occ[None]
    kernel = jnp.transpose(kernel_spectrum, (0, 2, 1))

    def rate(field):
        padded = with_halo(field, (("tx", 1), (TY, 2)), 1)
        effective = demag(field, kernel) + STIFFNESS * rim_sum(padded)
        torque = cross(field, effective)
        return -(torque + DAMPING * cross(field, torque)) / (1.0 + DAMPING * DAMPING)

    def normal(vector):
        return vector / jnp.sqrt(jnp.sum(vector * vector, axis=0) + 1.0 - occ)[None]

    first = rate(start)
    middle = normal(start + TIME_STEP * first)
    second = rate(middle)
    second = second - jnp.sum(second * start, axis=0)[None] * start
    mean_rate = 0.5 * (first + second)
    mag_next = normal(start + TIME_STEP * mean_rate)
    return (mag_next, mean_rate)


def solution(mesh):
    finer = Mesh(mesh.devices.reshape(mesh.shape["tx"], 4, 2), ("tx", "ty_0", "ty_1"))
    return jax.shard_map(
        body,
        mesh=finer,
        in_specs=(P(None, "tx", TY), P("tx", TY), P(None, TX_TY, None)),
        out_specs=(P(None, "tx", TY), P(None, "tx", TY)),
        check_vma=False,
    )
```

profile of v0, /device:TPU:1, one launch (start us, length us, event | category | flops | bytes accessed | tf_op | source)
XLA Modules:
  0.0 991.6 jit_solution(11731780759489699943)
XLA Ops:
  57.4 15.4 %all_to_all.70 = f32[16,128,192]{0,2,1:T(8,128)} reshape(f32[16,64,64,6]{0,3,2,1:T(8,128)} %copy.319) | data formatting | bytes 3145728 | tf_op jit(solution)/shard_map/all_to_all | solution.py:181
  93.8 27.6 %all-to-all-done.2 = f32[16,128,192]{2,0,1:T(8,128)S(1)} async-done(((f32[16,128,192]{2,0,1:T(8,128)}), f32[16,128,192]{2,0,1:T(8,128)S(1)}, u32[]{:S(2)}, u32[]{:S(2)}) %all-to-all-start.2) | async-done | bytes 1572896 | tf_op jit(solution)/shard_map/all_to_all | solution.py:181
  128.6 9.4 reshape_reshape.31
  171.2 17.7 %copy.325 = f32[64,64,192]{2,0,1:T(8,128)} copy(f32[64,64,192]{1,0,2:T(8,128)} %bitcast.308) | data formatting | bytes 6291456 | tf_op jit(solution)/shard_map/reshape | solution.py:84
  206.4 15.7 %fusion.6 = f32[64,64,192]{2,0,1:T(8,128)S(1)} fusion(f32[64,64,192]{1,0,2:T(8,128)S(1)} %bitcast.310), kind=kOutput, calls=%fused_computation.16 | convolution fusion | flops 604037120 | bytes 6291456 | tf_op jit(solution)/shard_map/cbz,bd->dcz/dot_general | solution.py:65
  330.9 13.6 %fusion.4 = f32[32,64,192]{2,0,1:T(8,128)S(1)} fusion(f32[64,64,192]{1,0,2:T(8,128)S(1)} %bitcast.315), kind=kOutput, calls=%fused_computation.14 | convolution fusion | flops 302018560 | bytes 4718592 | tf_op jit(solution)/shard_map/bcz,ca->abz/dot_general | solution.py:65
  350.5 34.6 %all_to_all.99 = f32[128,16,192]{2,1,0:T(8,128)S(1)} all-to-all(f32[128,16,192]{2,1,0:T(8,128)S(1)} %bitcast.351), channel_id=1, replica_groups=mesh['tx'=16,'ty_0'=4,'ty_1'=2] {'tx','ty_0','ty_1'}, dimensions={0} | all-to-all | bytes 3145728 | tf_op jit(solution)/shard_map/all_to_all | solution.py:185
  392.3 15.0 %reshape.305 = f32[16,64,64,6]{0,3,2,1:T(8,128)} reshape(f32[16,128,192]{0,2,1:T(8,128)} %copy.338) | data formatting | bytes 3145728 | tf_op jit(solution)/shard_map/reshape | solution.py:146
  407.3 15.7 %fusion.305 = (f32[16,64,64,3,1]{0,4,3,2,1:T(1,128)}, f32[16,64,64,3,1]{0,4,3,2,1:T(1,128)}) fusion(f32[16,64,64,3,2]{0,4,3,2,1:T(2,128)} %bitcast.303), kind=kLoop, calls=%fused_computation.399 | loop fusion | bytes 3145728 | tf_op jit(solution)/shard_map/slice | solution.py:84
  423.0 13.3 %copy.401 = f32[16,64,64,3,1]{2,1,4,3,0:T(8,128)S(1)} copy(f32[16,64,64,3,1]{0,4,3,2,1:T(1,128)} %get-tuple-element.16) | data formatting | bytes 1572864
  437.6 15.0 %copy.342 = f32[16,64,64,3,1]{2,1,4,3,0:T(8,128)} copy(f32[16,64,64,3,1]{0,4,3,2,1:T(1,128)} %get-tuple-element.17) | data formatting | bytes 1572864 | tf_op jit(solution)/shard_map/slice | solution.py:84
  452.6 9.7 copy.339
  508.8 10.7 %all_to_all.102 = f32[4,2,3,16,256]{4,1,3,2,0:T(2,128)S(1)} all-to-all(f32[4,2,3,16,256]{4,1,3,2,0:T(2,128)S(1)} %copy.352), channel_id=1, replica_groups=mesh['tx'=16,'ty_0'=4,'ty_1'=2] {'ty_0'}, dimensions={0} | all-to-all | bytes 786432 | tf_op jit(solution)/shard_map/all_to_all | solution.py:34
  555.8 15.4 %all_to_all.79 = f32[16,128,192]{0,2,1:T(8,128)} reshape(f32[16,64,64,6]{0,3,2,1:T(8,128)} %copy.358) | data formatting | bytes 3145728 | tf_op jit(solution)/shard_map/all_to_all | solution.py:181
  580.1 37.0 %all_to_all.103 = f32[16,128,192]{2,0,1:T(8,128)S(1)} all-to-all(f32[16,128,192]{2,0,1:T(8,128)} %copy.359), channel_id=1, replica_groups=mesh['tx'=16,'ty_0'=4,'ty_1'=2] {'tx','ty_0','ty_1'}, dimensions={1} | all-to-all | bytes 3145728 | tf_op jit(solution)/shard_map/all_to_all | solution.py:181
  624.4 9.4 reshape_reshape.36
  692.4 15.5 %fusion.2 = f32[64,64,192]{2,0,1:T(8,128)S(1)} fusion(f32[64,64,192]{1,0,2:T(8,128)S(1)} %bitcast.319), kind=kOutput, calls=%fused_computation.12 | convolution fusion | flops 604037120 | bytes 6291456 | tf_op jit(solution)/shard_map/cbz,bd->dcz/dot_general | solution.py:65
  816.9 13.3 %fusion = f32[32,64,192]{2,0,1:T(8,128)S(1)} fusion(f32[64,64,192]{1,0,2:T(8,128)S(1)} %bitcast.324), kind=kOutput, calls=%fused_computation.10 | convolution fusion | flops 302018560 | bytes 4718592 | tf_op jit(solution)/shard_map/bcz,ca->abz/dot_general | solution.py:65
  836.3 34.6 %all_to_all.104 = f32[128,16,192]{2,1,0:T(8,128)S(1)} all-to-all(f32[128,16,192]{2,1,0:T(8,128)S(1)} %bitcast.352), channel_id=1, replica_groups=mesh['tx'=16,'ty_0'=4,'ty_1'=2] {'tx','ty_0','ty_1'}, dimensions={0} | all-to-all | bytes 3145728 | tf_op jit(solution)/shard_map/all_to_all | solution.py:185
  878.1 15.0 %reshape.330 = f32[16,64,64,6]{0,3,2,1:T(8,128)} reshape(f32[16,128,192]{0,2,1:T(8,128)} %copy.377) | data formatting | bytes 3145728 | tf_op jit(solution)/shard_map/reshape | solution.py:146
  893.1 15.7 %fusion.304 = (f32[16,64,64,3,1]{0,4,3,2,1:T(1,128)}, f32[16,64,64,3,1]{0,4,3,2,1:T(1,128)}) fusion(f32[16,64,64,3,2]{0,4,3,2,1:T(2,128)} %bitcast.304), kind=kLoop, calls=%fused_computation.398 | loop fusion | bytes 3145728 | tf_op jit(solution)/shard_map/slice | solution.py:84
  908.8 13.3 %copy.404 = f32[16,64,64,3,1]{2,1,4,3,0:T(8,128)S(1)} copy(f32[16,64,64,3,1]{0,4,3,2,1:T(1,128)} %get-tuple-element.14) | data formatting | bytes 1572864
  923.4 15.0 %copy.381 = f32[16,64,64,3,1]{2,1,4,3,0:T(8,128)} copy(f32[16,64,64,3,1]{0,4,3,2,1:T(1,128)} %get-tuple-element.15) | data formatting | bytes 1572864 | tf_op jit(solution)/shard_map/slice | solution.py:84
  938.4 9.8 copy.378
  (278 shorter events, 581.6 us)
Async XLA Ops:
  9.8 12.3 %all-to-all-start.1 = ((f32[4,2,3,16,256]{4,1,3,2,0:T(2,128)}), f32[4,2,3,16,256]{4,1,3,2,0:T(2,128)S(1)}, u32[]{:S(2)}, u32[]{:S(2)}) async-start(f32[4,2,3,16,256]{4,1,3,2,0:T(2,128)} %copy.311), calls=%async_computation.1 | async-start | bytes 786432 | tf_op jit(solution)/shard_map/all_to_all | solution.py:34
  15.1 24.8 %copy-start.37 = (f32[64,64]{1,0:T(8,128)}, f32[64,64]{1,0:T(8,128)S(1)}, u32[]{:S(2)}) copy-start(f32[64,64]{1,0:T(8,128)S(1)} %copy.315) | copy-start | bytes 49156
  15.2 24.7 %copy-start.40 = (f32[64,64]{1,0:T(8,128)}, f32[64,64]{1,0:T(8,128)S(1)}, u32[]{:S(2)}) copy-start(f32[64,64]{1,0:T(8,128)S(1)} %copy.317) | copy-start | bytes 49156
  82.0 39.5 %all-to-all-start.2 = ((f32[16,128,192]{2,0,1:T(8,128)}), f32[16,128,192]{2,0,1:T(8,128)S(1)}, u32[]{:S(2)}, u32[]{:S(2)}) async-start(f32[16,128,192]{2,0,1:T(8,128)} %copy.320), calls=%async_computation.2 | async-start | bytes 4194304 | tf_op jit(solution)/shard_map/all_to_all | solution.py:181
  206.4 15.7 %copy-start = (f32[64,64,192]{2,0,1:T(8,128)S(1)}, f32[64,64,192]{2,0,1:T(8,128)}, u32[]{:S(2)}) copy-start(f32[64,64,192]{2,0,1:T(8,128)} %multiply_subtract_fusion.1) | copy-start | bytes 9437188
  330.9 13.6 %copy-start.3 = (f32[64,64,192]{2,0,1:T(8,128)S(1)}, f32[64,64,192]{2,0,1:T(8,128)}, u32[]{:S(2)}) copy-start(f32[64,64,192]{2,0,1:T(8,128)} %multiply_add_fusion.1) | copy-start | bytes 9437188
  475.9 9.7 copy-start.7
  482.1 16.1 %all-to-all-start.4 = ((f32[4,2,3,16,256]{4,1,2,3,0:T(2,128)}), f32[4,2,3,16,256]{4,1,2,3,0:T(2,128)S(1)}, u32[]{:S(2)}, u32[]{:S(2)}) async-start(f32[4,2,3,16,256]{4,1,2,3,0:T(2,128)} %copy.346), calls=%async_computation.4 | async-start | bytes 786432 | tf_op jit(solution)/shard_map/all_to_all | solution.py:34
  485.6 16.8 %collective-permute-start = (f32[3,1,256]{2,1,0:T(1,128)S(1)}, f32[3,1,256]{2,1,0:T(1,128)S(1)}, u32[]{:S(2)}, u32[]{:S(2)}) collective-permute-start(f32[3,1,256]{2,1,0:T(1,128)S(1)} %get-tuple-element.73), channel_id=1, source_target_pairs={{8,0},{16,8},{24,16},{32,24},{40,32},{48,40},{56,48},{64,56},{72,6... | collective-permute-start | bytes 9224 | tf_op jit(solution)/shard_map/ppermute | solution.py:53
  486.9 15.5 %collective-permute-start.1 = (f32[3,1,256]{2,1,0:T(1,128)S(1)}, f32[3,1,256]{2,1,0:T(1,128)S(1)}, u32[]{:S(2)}, u32[]{:S(2)}) collective-permute-start(f32[3,1,256]{2,1,0:T(1,128)S(1)} %get-tuple-element.72), channel_id=1, source_target_pairs={{0,8},{8,16},{16,24},{24,32},{32,40},{40,48},{48,56},{56,64},{64,7... | collective-permute-start | bytes 9224 | tf_op jit(solution)/shard_map/ppermute | solution.py:52
  491.0 11.4 %collective-permute-start.2 = (f32[3,128,1]{2,1,0:T(8,128)S(1)}, f32[3,128,1]{2,1,0:T(8,128)S(1)}, u32[]{:S(2)}, u32[]{:S(2)}) collective-permute-start(f32[3,128,1]{2,1,0:T(8,128)S(1)} %get-tuple-element.70), channel_id=1, source_target_pairs={{1,0},{2,1},{3,2},{4,3},{5,4},{6,5},{7,6},{9,8},{10,9},{11,10},{12... | collective-permute-start | bytes 4616 | tf_op jit(solution)/shard_map/ppermute | solution.py:53
  494.7 7.7 collective-permute-start.3
  502.9 5.9 copy-start.27
  502.9 5.9 copy-start.33
  503.0 16.5 %copy-start.31 = (f32[1,128,256]{2,1,0:T(8,128)}, f32[1,128,256]{2,1,0:T(8,128)S(1)}, u32[]{:S(2)}) copy-start(f32[1,128,256]{2,1,0:T(8,128)S(1)} %multiply_subtract_fusion.10) | copy-start | bytes 393220
  692.4 15.5 %copy-start.1 = (f32[64,64,192]{2,0,1:T(8,128)S(1)}, f32[64,64,192]{2,0,1:T(8,128)}, u32[]{:S(2)}) copy-start(f32[64,64,192]{2,0,1:T(8,128)} %multiply_subtract_fusion) | copy-start | bytes 9437188
  765.8 5.9 copy-start.11
  816.9 13.3 %copy-start.2 = (f32[64,64,192]{2,0,1:T(8,128)S(1)}, f32[64,64,192]{2,0,1:T(8,128)}, u32[]{:S(2)}) copy-start(f32[64,64,192]{2,0,1:T(8,128)} %multiply_add_fusion) | copy-start | bytes 9437188
  961.7 9.5 copy-start.9
  967.8 16.1 %all-to-all-start.10 = ((f32[4,2,3,16,256]{4,1,2,3,0:T(2,128)}), f32[4,2,3,16,256]{4,1,2,3,0:T(2,128)S(1)}, u32[]{:S(2)}, u32[]{:S(2)}) async-start(f32[4,2,3,16,256]{4,1,2,3,0:T(2,128)} %copy.385), calls=%async_computation.10 | async-start | bytes 786432 | tf_op jit(solution)/shard_map/all_to_all | solution.py:34
  971.3 16.8 %collective-permute-start.4 = (f32[3,1,256]{2,1,0:T(1,128)S(1)}, f32[3,1,256]{2,1,0:T(1,128)S(1)}, u32[]{:S(2)}, u32[]{:S(2)}) collective-permute-start(f32[3,1,256]{2,1,0:T(1,128)S(1)} %get-tuple-element.69), channel_id=1, source_target_pairs={{8,0},{16,8},{24,16},{32,24},{40,32},{48,40},{56,48},{64,56},{72,6... | collective-permute-start | bytes 9224 | tf_op jit(solution)/shard_map/ppermute | solution.py:53
  972.6 15.5 %collective-permute-start.5 = (f32[3,1,256]{2,1,0:T(1,128)S(1)}, f32[3,1,256]{2,1,0:T(1,128)S(1)}, u32[]{:S(2)}, u32[]{:S(2)}) collective-permute-start(f32[3,1,256]{2,1,0:T(1,128)S(1)} %get-tuple-element.68), channel_id=1, source_target_pairs={{0,8},{8,16},{16,24},{24,32},{32,40},{40,48},{48,56},{56,64},{64,7... | collective-permute-start | bytes 9224 | tf_op jit(solution)/shard_map/ppermute | solution.py:52
  976.7 11.4 %collective-permute-start.6 = (f32[3,128,1]{2,1,0:T(8,128)S(1)}, f32[3,128,1]{2,1,0:T(8,128)S(1)}, u32[]{:S(2)}, u32[]{:S(2)}) collective-permute-start(f32[3,128,1]{2,1,0:T(8,128)S(1)} %get-tuple-element.66), channel_id=1, source_target_pairs={{1,0},{2,1},{3,2},{4,3},{5,4},{6,5},{7,6},{9,8},{10,9},{11,10},{12... | collective-permute-start | bytes 4616 | tf_op jit(solution)/shard_map/ppermute | solution.py:53
  980.4 7.8 collective-permute-start.7
  (31 other events, 89.1 us)
where the time goes:
time: 1010 us; the launch traced here: 992 us
  local copies, waits for them, and re-layouts  471 us (47%)
  matrix products  179 us (18%)
  blocking collectives  134 us (13%)
  other arithmetic  124 us (12%)
  starting transfers between devices  45.8 us (5%)
  waiting for transfers between devices  34.6 us (3%)
    dot_general x32, matrix products, contract(): return jnp.einsum(form, left, right, precision=lax.Precision.HIGHEST)  179 us
    all_to_all x2, blocking collectives, send_back(): lax.all_to_all(partial_value, TX_TY, split_axis=0, concat_axis=1, tiled=T...  69.2 us
    reshape x8, local copies, waits for them, and re-layouts, turn(): jnp.stack([-paired[..., 1], paired[..., 0]], axis=-1).reshape(values.shape)  65.1 us
    all_to_all x6, local copies, waits for them, and re-layouts, send_out(): lax.all_to_all(spectra, TX_TY, split_axis=1, concat_axis=0, tiled=True)  63.4 us
    reshape x4, local copies, waits for them, and re-layouts, y_inverse(): shaped = spectra.reshape(row_count, second_len, first_len, 6)  49.6 us
    neg x18, other arithmetic, turn(): -paired[..., 1]  43.8 us
    all_to_all x1, blocking collectives, send_out(): lax.all_to_all(spectra, TX_TY, split_axis=1, concat_axis=0, tiled=True)  37 us
    another operation x18, other arithmetic, turn(): jnp.stack([-paired[..., 1], paired[..., 0]], axis=-1).reshape(values.shape)  34.1 us
  transfers between devices with their start and end apart: 12, of which 2 were waited for; matrix products, arithmetic and copies ran while one was open for 0% of the time, Pallas kernels for 0%

commit v1 on v0

v1 whole, which is shorter than its diff:
```python
import functools
import math

import jax
import jax.numpy as jnp
import ml_dtypes
import numpy as np
from jax import lax
from jax.experimental import pallas as pl
from jax.experimental.pallas import tpu as pltpu
from jax.sharding import PartitionSpec as P

DAMPING = 0.3
STIFFNESS = 0.25
TIME_STEP = 0.25
MESH = pl.DeviceIdType.MESH
F32 = jnp.float32
BF16 = jnp.bfloat16


(T_WA, T_WAQ, T_W1R, T_W1I, T_W2, T_W2I, T_BR, T_BI, T_W3, T_W3Q, T_S2, T_S2I) = (
    0, 1, 2, 3, 4, 5, 6, 7, 8, 9, 10, 13,
)
N_TABLES = 16


def angle(left, right, length):
    product = np.arange(left)[:, None] * np.arange(right)[None, :] % length
    return 2.0 * math.pi * product / length


def matrices():
    out = np.zeros((N_TABLES, 256, 256))
    th = angle(128, 128, 128)
    cos, sin = np.cos(th), np.sin(th)
    out[T_WA] = np.block([[cos, sin], [-sin, cos]])
    scale = -(2.0**-24)
    out[T_W3] = 2.0 * scale * np.block([[cos, sin], [-sin, cos]])
    ph = th + 2.0 * math.pi * np.arange(128)[None, :] / 256.0
    low, high = np.arange(1, 64), np.arange(64, 128)
    sign = 1.0 - 2.0 * (np.arange(128) % 2)
    q = np.zeros((2, 128, 2, 128))
    q[0, 0, 0], q[1, 0, 0] = 1.0, sign
    q[0, low, 0], q[1, low, 0] = cos[low], -sin[low]
    q[0, high, 1], q[1, high, 1] = np.cos(ph)[high], -np.sin(ph)[high]
    out[T_WAQ] = q.reshape(256, 256)
    weight = np.full((128, 1, 1), 2.0)
    weight[0] = 1.0
    out[T_W3Q] = scale * (q * weight).reshape(256, 256)
    th = angle(256, 128, 256)
    cos, sin = np.cos(th), np.sin(th)
    out[T_W1R] = np.concatenate([cos, sin], 1)
    out[T_W1I] = np.concatenate([-sin, cos], 1)
    out[T_BR] = np.concatenate([cos.T, sin.T], 0)
    out[T_BI] = np.concatenate([-sin.T, cos.T], 0)
    th = angle(16, 16, 16)
    cos, sin = np.cos(th), np.sin(th)
    eight = np.eye(8)
    wc = np.einsum("ab,id->aidb", eight, cos).reshape(128, 128)
    ws = np.einsum("ab,id->aidb", eight, sin).reshape(128, 128)
    out[T_W2] = np.block([[wc, -ws], [ws, wc]])
    out[T_W2I] = np.block([[wc.T, ws.T], [-ws.T, wc.T]])
    for m in range(3):
        sc, ss = np.zeros((128, 128)), np.zeros((128, 128))
        for j in range(2):
            rows = slice(48 * j + 16 * m, 48 * j + 16 * m + 16)
            cols = slice(16 * j, 16 * j + 16)
            sc[rows, cols], ss[rows, cols] = cos, sin
        out[T_S2 + m] = np.block([[sc, -ss], [ss, sc]])
        out[T_S2I + m] = np.block([[sc.T, ss.T], [-ss.T, sc.T]])
    return out


def two_parts(value):
    high = value.astype(np.float32).astype(ml_dtypes.bfloat16)
    low = (value - high.astype(np.float64)).astype(np.float32).astype(ml_dtypes.bfloat16)
    return np.stack([high, low])


def twiddles():
    th = 2.0 * math.pi * (np.arange(256)[:, None] * (np.arange(128) % 16)[None, :]) / 4096.0
    ty = angle(16, 128, 4096)
    return np.concatenate([np.cos(th), np.sin(th), np.cos(ty), np.sin(ty)], 0).astype(np.float32)


def split(value):
    high = value.astype(BF16)
    return high, (value - high.astype(F32)).astype(BF16)


def product(a, b, form=(((1,), (0,)), ((), ()))):
    dot = functools.partial(lax.dot_general, dimension_numbers=form, preferred_element_type=F32)
    return dot(a[0], b[0]) + (dot(a[0], b[1]) + dot(a[1], b[0]))


LANES = (((1,), (1,)), ((), ()))


def cross(left, right):
    return [
        left[1] * right[2] - left[2] * right[1],
        left[2] * right[0] - left[0] * right[2],
        left[0] * right[1] - left[1] * right[0],
    ]


def squared(v):
    return v[0] * v[0] + v[1] * v[1] + v[2] * v[2]


def kernel(n_tx, n_ty, mag_h, occ_h, ks_h, cb_h, tw_h, next_ref, rate_ref, mag, occ, ks, cb, tw, m0l, fb, k1, dm, ex,
           mr, mrl, hb, kt, kr, kr2, kst, s1, r1, s2, r2, u, uq, oq, zb, xs, ys, pb, os, load_sem, ty_send, ty_recv,
           h_send, h_recv, k_send, k_recv, a_send, a_recv, b_send, b_recv, f_send, f_recv):
    n = n_tx * n_ty
    tx, ty = lax.axis_index("tx"), lax.axis_index("ty")
    me = tx * n_ty + ty

    loads = [
        pltpu.make_async_copy(mag_h, mag, load_sem.at[0]),
        pltpu.make_async_copy(occ_h, occ, load_sem.at[1]),
        pltpu.make_async_copy(ks_h.at[:, pl.ds(0, 24), :], ks, load_sem.at[2]),
        pltpu.make_async_copy(cb_h, cb, load_sem.at[3]),
        pltpu.make_async_copy(tw_h, tw, load_sem.at[4]),
    ]
    for load in loads:
        load.start()

    barrier = pltpu.get_barrier_semaphore()

    def greet(p, _):
        to = lax.rem(me + p, n)
        pl.semaphore_signal(barrier, inc=1, device_id=(to // n_ty, lax.rem(to, n_ty)), device_id_type=MESH)
        return 0

    lax.fori_loop(1, n, greet, 0)
    loads[0].wait()
    loads[1].wait()
    occf = occ[...].astype(F32)
    for m in range(3):
        m0l[m] = mag[m] * occf
    pl.semaphore_wait(barrier, n - 1)

    def table(k):
        return cb[0, k], cb[1, k]

    mine = pl.ds(pl.multiple_of(ty * 256, 256), 256)

    def ty_out(p, _):
        to = lax.rem(ty + p, n_ty)
        pltpu.make_async_remote_copy(
            src_ref=m0l.at[:, pl.ds(pl.multiple_of(to * 16, 16), 16), :], dst_ref=fb.at[0, :, :, mine],
            send_sem=ty_send, recv_sem=ty_recv, device_id=(tx, to), device_id_type=MESH,
        ).start()
        return 0

    lax.fori_loop(1, n_ty, ty_out, 0)
    own_rows = pl.ds(pl.multiple_of(ty * 16, 16), 16)
    pltpu.make_async_copy(m0l.at[:, own_rows, :], fb.at[0, :, :, mine], ty_recv).start()

    loads[2].wait()
    upper = me >= n // 2
    top = lax.broadcasted_iota(jnp.int32, (8, 256), 0) == 0
    for k in range(4):
        for h in range(2):
            tiles = []
            for d in range(16):
                tile = ks[k, pl.ds(8 * h, 8), pl.ds(256 * d, 256)]
                if h == 0:
                    kr[k, pl.ds(d, 1), :] = ks[k, pl.ds(0, 1), pl.ds(256 * d, 256)]
                    other = ks[k, pl.ds(16, 8), pl.ds(256 * d, 256)]
                    tile = jnp.where(jnp.logical_and(top, upper), other, tile)
                tiles.append(tile)
            kt[k, h] = jnp.concatenate(tiles, 0).T

    def row_copy():
        return pltpu.make_async_remote_copy(
            src_ref=kr, dst_ref=kr2, send_sem=k_send, recv_sem=k_recv, device_id=(0, 0), device_id_type=MESH
        )

    @pl.when(me == n // 2)
    def _():
        row_copy().start()
        row_copy().wait_send()

    loads[3].wait()
    loads[4].wait()
    uq[...] = jnp.zeros_like(uq)

    @pl.when(me == 0)
    def _():
        row_copy().wait_recv()
        for k in range(4):
            rows = jnp.concatenate([kr[k], kr2[k], jnp.zeros((96, 256), F32)], 0)
            kst[k] = rows.T

    pltpu.make_async_copy(fb.at[0], fb.at[0], ty_recv).wait()
    rest = m0l.at[:, pl.ds(0, 16 * (n_ty - 1)), :]
    pltpu.make_async_copy(rest, rest, ty_send).wait()

    def exchange(source, target, send, recv):
        own = pl.ds(pl.multiple_of(me * 4, 4), 4)

        def out(p, _):
            to = lax.rem(me + p, n)
            pltpu.make_async_remote_copy(
                src_ref=source.at[:, pl.ds(pl.multiple_of(to * 4, 4), 4), :], dst_ref=target.at[:, own, :],
                send_sem=send, recv_sem=recv, device_id=(to // n_ty, lax.rem(to, n_ty)), device_id_type=MESH,
            ).start()
            return 0

        lax.fori_loop(1, n, out, 0)
        pltpu.make_async_copy(source.at[:, own, :], target.at[:, own, :], recv).start()

    def arrived(target, recv):
        pltpu.make_async_copy(target, target, recv).wait()

    def sent(source, send):
        rest = source.at[:, pl.ds(0, 4 * (n - 1)), :]
        pltpu.make_async_copy(rest, rest, send).wait()

    lane = lax.broadcasted_iota(jnp.int32, (128, 128), 1)
    after, before = lax.rem(me + 1, n), lax.rem(me + n - 1, n)

    def step(it, _):
        halos = []
        for side, (to, row) in enumerate(((after, 15), (before, 0))):
            halos.append(pltpu.make_async_remote_copy(
                src_ref=fb.at[it, :, row], dst_ref=hb.at[it, side, pl.ds(0, 3)],
                send_sem=h_send.at[side], recv_sem=h_recv.at[it, side],
                device_id=(to // n_ty, lax.rem(to, n_ty)), device_id_type=MESH,
            ))
        for halo in halos:
            halo.start()

        def y_first(m, _):
            a = [fb[it, m, :, pl.ds(128 * k, 128)] for k in range(16)]
            real, imag = [None] * 17, [None] * 17
            for c in range(9):
                sums = []
                for odd in range(2):
                    re, im = None, None
                    for k in range(odd, 16, 2):
                        w = 2.0 * math.pi * (c * k % 32) / 32.0
                        wr, wi = round(math.cos(w), 15), round(-math.sin(w), 15)
                        if wr != 0.0:
                            re = a[k] * wr if re is None else re + a[k] * wr
                        if wi != 0.0:
                            im = a[k] * wi if im is None else im + a[k] * wi
                    zero = jnp.zeros_like(a[0])
                    sums.append((zero if re is None else re, zero if im is None else im))
                (er, ei), (ro, io) = sums
                real[c], imag[c] = er + ro, ei + io
                real[16 - c], imag[16 - c] = er - ro, io - ei
            base = pl.multiple_of(m * 256, 256)
            for c in range(16):
                if c == 0:
                    vr, vi = real[0], real[16]
                else:
                    cos, sin = tw[pl.ds(512 + c, 1), :], tw[pl.ds(528 + c, 1), :]
                    vr, vi = real[c] * cos + imag[c] * sin, imag[c] * cos - real[c] * sin
                for part, v in enumerate((vr, vi)):
                    cols = pl.ds(128 * part, 128)
                    for k, piece in enumerate(split(v)):
                        u[k, pl.ds(base + 16 * c, 16), cols] = piece
                        if c == 0:
                            uq[k, pl.ds(pl.multiple_of(m * 16, 16), 16), cols] = piece
            return 0

        lax.fori_loop(0, 3, y_first, 0)
        oq[...] = product(table(T_WAQ), (uq[0], uq[1]), LANES)

        @pl.when(it == 1)
        def _():
            sent(s1, a_send)

        def y_second(m, _):
            rows = pl.ds(pl.multiple_of(m * 256, 256), 256)
            full = product(table(T_WA), (u[0, rows], u[1, rows]), LANES)
            for part in range(2):
                block = full[128 * part:128 * part + 128]
                own = pltpu.roll(oq[pl.ds(128 * part, 128), :], lax.rem(128 - 16 * m, 128), 1)
                s1[m, pl.ds(2 * part, 128, stride=4), :] = jnp.where(lane < 16, own, block[:, :128])
                s1[m, pl.ds(2 * part + 1, 128, stride=4), :] = block[:, 128:]
            return 0

        lax.fori_loop(0, 3, y_second, 0)
        exchange(s1, r1, a_send, a_recv)

        for halo in halos:
            halo.wait_recv()
        row = lax.broadcasted_iota(jnp.int32, (16, 2048), 0)
        col = lax.broadcasted_iota(jnp.int32, (16, 2048), 1)
        for m in range(3):
            f = fb[it, m]
            low = jnp.where(me > 0, hb[it, 0, pl.ds(m, 1), :], 0.0)
            high = jnp.where(me < n - 1, hb[it, 1, pl.ds(m, 1), :], 0.0)
            up = jnp.where(row == 0, low, pltpu.roll(f, 1, 0))
            down = jnp.where(row == 15, high, pltpu.roll(f, 15, 0))
            left = jnp.where(col == 0, 0.0, pltpu.roll(f, 1, 1))
            right = jnp.where(col == 2047, 0.0, pltpu.roll(f, 2047, 1))
            ex[m] = STIFFNESS * (down + up + right + left)
        for halo in halos:
            halo.wait_send()

        arrived(r1, a_recv)

        def x_forward(m, _):
            for part in range(2):
                for h in range(2):
                    block = r1[m, pl.ds(2 * part + h, 128, stride=4), :]
                    for k, piece in enumerate(split(block)):
                        xs[k, pl.ds(128 * part, 128), pl.ds(128 * h, 128)] = piece
            x = (xs[0], xs[1])
            tr, ti = product(table(T_W1R), x), product(table(T_W1I), x)
            cos, sin = tw[pl.ds(0, 256), :], tw[pl.ds(256, 256), :]
            for h in range(2):
                ar, ai = tr[:, 128 * h:128 * h + 128], ti[:, 128 * h:128 * h + 128]
                v = jnp.concatenate([ar * cos + ai * sin, ai * cos - ar * sin], 1)
                z = product(split(v), table(T_W2))
                zb[m, h, 0] = z[:, :128]
                zb[m, h, 1] = z[:, 128:]
            return 0

        lax.fori_loop(0, 3, x_forward, 0)

        @pl.when(me == 0)
        def _():
            cos, sin = tw[pl.ds(0, 256), :], tw[pl.ds(256, 256), :]
            seq = jnp.zeros((128, 128), F32)
            for j in range(2):
                for m in range(3):
                    block = r1[m, pl.ds(2 * j, 128, stride=4), :]
                    place = 48 * j + 16 * m
                    inside = jnp.logical_and(lane >= place, lane < place + 16)
                    seq = jnp.where(inside, pltpu.roll(block, place, 1) if place else block, seq)
            seq = split(seq)
            ar = product((cb[0, T_W1R][:, :128], cb[1, T_W1R][:, :128]), seq)
            ai = product((cb[0, T_W1I][:, :128], cb[1, T_W1I][:, :128]), seq)
            v = split(jnp.concatenate([ar * cos + ai * sin, ai * cos - ar * sin], 1))
            z = [product(v, table(T_S2 + m)) for m in range(3)]
            two = lambda k: jnp.concatenate([kst[k], kst[k]], 1)
            xx, yy, zz, xy = two(0), two(1), two(2), two(3)
            field = [xx * z[0] + xy * z[1], xy * z[0] + yy * z[1], zz * z[2]]
            back = 0.0
            for m in range(3):
                back = back + product(split(field[m]), table(T_S2I + m))
            br, bi = back[:, :128], back[:, 128:]
            yr, yi = split(br * cos - bi * sin), split(bi * cos + br * sin)
            os[...] = product((cb[0, T_BR][:128], cb[1, T_BR][:128]), yr) + product(
                (cb[0, T_BI][:128], cb[1, T_BI][:128]), yi)

        def gains(k, _):
            h, part = k // 2, lax.rem(k, 2)
            x, y, z = zb[0, h, part], zb[1, h, part], zb[2, h, part]
            xy = kt[3, h]
            zb[0, h, part] = kt[0, h] * x + xy * y
            zb[1, h, part] = xy * x + kt[1, h] * y
            zb[2, h, part] = kt[2, h] * z
            return 0

        lax.fori_loop(0, 4, gains, 0)

        @pl.when(it == 1)
        def _():
            sent(s2, b_send)

        def x_inverse(m, _):
            cos, sin = tw[pl.ds(0, 256), :], tw[pl.ds(256, 256), :]
            for h in range(2):
                field = split(jnp.concatenate([zb[m, h, 0], zb[m, h, 1]], 1))
                p = product(field, table(T_W2I))
                pr, pi = p[:, :128], p[:, 128:]
                for part, v in enumerate((pr * cos - pi * sin, pi * cos + pr * sin)):
                    for k, piece in enumerate(split(v)):
                        ys[k, part, :, pl.ds(128 * h, 128)] = piece
            o = product(table(T_BR), (ys[0, 0], ys[1, 0])) + product(table(T_BI), (ys[0, 1], ys[1, 1]))
            for part in range(2):
                for h in range(2):
                    s2[m, pl.ds(2 * part + h, 128, stride=4), :] = (
                        o[128 * part:128 * part + 128, 128 * h:128 * h + 128])

            @pl.when(me == 0)
            def _():
                for j in range(2):
                    place = pl.ds(2 * j, 128, stride=4)
                    own = pltpu.roll(os[...], 128 - 48 * j - 16 * m, 1)
                    s2[m, place, :] = jnp.where(lane < 16, own, s2[m, place, :])

            return 0

        lax.fori_loop(0, 3, x_inverse, 0)
        exchange(s2, r2, b_send, b_recv)
        arrived(r2, b_recv)

        def y_inverse(m, _):
            for part in range(2):
                for h in range(2):
                    block = r2[m, pl.ds(2 * part + h, 128, stride=4), :].T
                    for k, piece in enumerate(split(block)):
                        xs[k, pl.ds(128 * h, 128), pl.ds(128 * part, 128)] = piece
            pb[...] = product((xs[0], xs[1]), table(T_W3))
            pq = product((xs[0, pl.ds(0, 16), :], xs[1, pl.ds(0, 16), :]), table(T_W3Q))
            real, imag = [None] * 16, [None] * 16
            for c in range(1, 16):
                cos, sin = tw[pl.ds(512 + c, 1), :], tw[pl.ds(528 + c, 1), :]
                br, bi = pb[pl.ds(16 * c, 16), pl.ds(0, 128)], pb[pl.ds(16 * c, 16), pl.ds(128, 128)]
                real[c], imag[c] = br * cos - bi * sin, bi * cos + br * sin
            ends = (pq[:, :128] + pq[:, 128:], pq[:, :128] - pq[:, 128:])
            pairs = []
            for odd in range(2):
                pairs.append([
                    (real[c] - real[16 - c], imag[c] + imag[16 - c]) if odd
                    else (real[c] + real[16 - c], imag[c] - imag[16 - c]) for c in range(1, 8)
                ])
            for a in range(16):
                total = ends[a % 2]
                for c in range(1, 9):
                    re, im = pairs[a % 2][c - 1] if c < 8 else (real[8], imag[8])
                    w = 2.0 * math.pi * (c * a % 32) / 32.0
                    wr, wi = round(math.cos(w), 15), round(math.sin(w), 15)
                    if wr != 0.0:
                        total = total + re * wr
                    if wi != 0.0:
                        total = total - im * wi
                dm[m, :, pl.ds(128 * a, 128)] = total
            return 0

        lax.fori_loop(0, 3, y_inverse, 0)

        def advance(j, _):
            cols = pl.ds(pl.multiple_of(j * 256, 256), 256)
            m0 = [fb[0, m, :, cols] for m in range(3)]
            f = [fb[it, m, :, cols] for m in range(3)]
            heff = [dm[m, :, cols] + ex[m, :, cols] for m in range(3)]
            torque = cross(f, heff)
            damped = cross(f, torque)
            rate = [(t + DAMPING * d) * (-1.0 / (1.0 + DAMPING * DAMPING)) for t, d in zip(torque, damped)]

            @pl.when(it == 0)
            def _():
                filled = jnp.where(squared(m0) > 0.5, 0.0, 1.0)
                v = [m + TIME_STEP * r for m, r in zip(m0, rate)]
                root = jnp.sqrt(squared(v) + filled)
                for m in range(3):
                    k1[m, :, cols] = rate[m]
                    fb[1, m, :, cols] = v[m] / root

            @pl.when(it == 1)
            def _():
                along = rate[0] * m0[0] + rate[1] * m0[1] + rate[2] * m0[2]
                for m in range(3):
                    mr[m, :, cols] = 0.5 * (k1[m, :, cols] + (rate[m] - along * m0[m]))

            return 0

        lax.fori_loop(0, 8, advance, 0)
        return 0

    lax.fori_loop(0, 2, step, 0)
    sent(s1, a_send)
    sent(s2, b_send)

    def back(p, _):
        to = lax.rem(ty + p, n_ty)
        pltpu.make_async_remote_copy(
            src_ref=mr.at[:, :, pl.ds(pl.multiple_of(to * 256, 256), 256)], dst_ref=mrl.at[:, own_rows, :],
            send_sem=f_send, recv_sem=f_recv, device_id=(tx, to), device_id_type=MESH,
        ).start()
        return 0

    lax.fori_loop(1, n_ty, back, 0)
    pltpu.make_async_copy(mr.at[:, :, mine], mrl.at[:, own_rows, :], f_recv).start()
    pltpu.make_async_copy(mrl, mrl, f_recv).wait()
    pltpu.make_async_copy(rest, rest, f_send).wait()

    def finish(j, _):
        rows = pl.ds(pl.multiple_of(j * 16, 16), 16)
        r = [mrl[m, rows, :] for m in range(3)]
        v = [m0l[m, rows, :] + TIME_STEP * r[m] for m in range(3)]
        root = jnp.sqrt(squared(v) + 1.0 - occ[rows, :].astype(F32))
        for m in range(3):
            rate_ref[m, rows, :] = r[m]
            next_ref[m, rows, :] = v[m] / root
        return 0

    lax.fori_loop(0, 8, finish, 0)


def body(n_tx, n_ty, mag, occupancy, kernel_spectrum):
    cb = jnp.asarray(two_parts(matrices()))
    tw = jnp.asarray(twiddles())
    V = pltpu.VMEM
    D = pltpu.SemaphoreType.DMA
    block = (3, 128, 256)
    band = (3, 16, 2048)
    slots = (3, 512, 128)
    out = jax.ShapeDtypeStruct(block, F32)
    return pl.pallas_call(
        functools.partial(kernel, n_tx, n_ty),
        out_shape=(out, out),
        in_specs=[pl.BlockSpec(memory_space=pl.ANY)] * 5,
        out_specs=(pl.BlockSpec(memory_space=pltpu.VMEM),) * 2,
        scratch_shapes=[
            V(block, F32), V((128, 256), jnp.int32), V((4, 24, 4096), F32), V((2, N_TABLES, 256, 256), BF16),
            V((544, 128), F32),
            V(block, F32), V((2,) + band, F32), V(band, F32), V(band, F32), V(band, F32),
            V(band, F32), V(block, F32), V((2, 2, 8, 2048), F32), V((4, 2, 256, 128), F32),
            V((4, 16, 256), F32), V((4, 16, 256), F32), V((4, 256, 128), F32),
            V(slots, F32), V(slots, F32), V(slots, F32), V(slots, F32),
            V((2, 768, 256), BF16), V((2, 128, 256), BF16), V((256, 128), F32), V((3, 2, 2, 256, 128), F32),
            V((2, 256, 256), BF16), V((2, 2, 256, 256), BF16), V((256, 256), F32), V((128, 128), F32),
            D((5,)), D, D, D((2,)), D((2, 2)), D, D, D, D, D, D, D, D,
        ],
        compiler_params=pltpu.CompilerParams(
            collective_id=0, has_side_effects=True, vmem_limit_bytes=56 * 1024 * 1024
        ),
    )(mag, occupancy, kernel_spectrum, cb, tw)


def solution(mesh):
    return jax.shard_map(
        functools.partial(body, mesh.shape["tx"], mesh.shape["ty"]),
        mesh=mesh,
        in_specs=(P(None, "tx", "ty"), P("tx", "ty"), P(None, ("tx", "ty"), None)),
        out_specs=(P(None, "tx", "ty"), P(None, "tx", "ty")),
        check_vma=False,
    )
```

time: 1010 us -> 104 us (0.10); the launches traced: 992 us -> 104 us
  local copies, waits for them, and re-layouts: 471 us -> 3.53 us
  matrix products: 179 us -> 0 us
  blocking collectives: 134 us -> 0 us
  other arithmetic: 124 us -> 0 us
  Pallas kernels: 0 us -> 99.7 us
  starting transfers between devices: 45.8 us -> 0 us
  waiting for transfers between devices: 34.6 us -> 0 us
    dot_general x32 -> x0, matrix products: 179 us -> none  [contract(): return jnp.einsum(form, left, right, precision=lax.Precision.HIGHEST)]
    all_to_all x8 -> x0, blocking collectives: 134 us -> none  [the longest x2 69.2 us: send_back(): lax.all_to_all(partial_value, TX_TY, split_axis=0, concat_axis=1, tiled=T...]
    reshape x16 -> x0, local copies, waits for them, and re-layouts: 117 us -> none  [the longest x8 65.1 us: turn(): jnp.stack([-paired[..., 1], paired[..., 0]], axis=-1).reshape(values.shape)]
    pallas_call x0 -> x1, Pallas kernels: none -> 99.7 us  [body(): pl.pallas_call(functools.partial(kernel, n_tx, n_ty), out_shape=(out, out...]
    another operation x18 -> x0, local copies, waits for them, and re-layouts: 85.6 us -> none  [the longest x4 29.2 us: turn(): paired = values.reshape(values.shape[:-1] + (values.shape[-1] // 2, 2))]
    all_to_all x14 -> x0, local copies, waits for them, and re-layouts: 79.8 us -> none  [the longest x6 63.4 us: send_out(): lax.all_to_all(spectra, TX_TY, split_axis=1, concat_axis=0, tiled=True)]
    slice x8 -> x0, local copies, waits for them, and re-layouts: 61.6 us -> none  [the longest x2 31.4 us: turn(): paired[..., 1]]
    sub x8 -> x0, local copies, waits for them, and re-layouts: 61.3 us -> none  [the longest x2 17.9 us: y_forward(): contract('rbcz,bd->rdcz', section, cos_two)]
  transfers between devices with their start and end apart: 12 -> 0, of which waited for: 2 -> 0; matrix products, arithmetic and copies ran while one was open for 0% -> 0% of each run, Pallas kernels for 0% -> 0%
where the time goes in v1:
time: 104 us
  Pallas kernels  99.7 us (96%)
  local copies, waits for them, and re-layouts  3.53 us (3%)
    pallas_call x1, Pallas kernels, body(): pl.pallas_call(functools.partial(kernel, n_tx, n_ty), out_shape=(out, out...  99.7 us
    unnamed x2, local copies, waits for them, and re-layouts  3.53 us

profile of v1, /device:TPU:1, one launch (start us, length us, event | category | flops | bytes accessed | tf_op | source)
XLA Modules:
  0.0 103.9 jit_solution(16337463731360501019)
XLA Ops:
  0.6 99.7 %shard_map.68 = (f32[3,128,256]{2,1,0:T(8,128)}, f32[3,128,256]{2,1,0:T(8,128)}) custom-call(f32[3,128,256]{2,1,0:T(8,128)} %mag_h.1, s32[128,256]{1,0:T(8,128)} %occ_h.1, f32[4,32,4096]{2,1,0:T(8,128)} %ks_h.1, bf16[2,16,256,256]{3,2,1,0:T(8,128)(2,1)} %constant.4.clone.cb_h, f32[544,128]{1,0:T(8,128)} %constant.5.clone.tw_h), custom_call_target="tpu_custom_call" | custom-call | tf_op jit(solution)/shard_map/pallas_call | solution.py:498
  100.4 1.8 %copy.9 = f32[3,128,256]{2,1,0:T(8,128)} copy(f32[3,128,256]{2,1,0:T(8,128)} %get-tuple-element.4) | data formatting | bytes 786432
  102.2 1.8 %copy.10 = f32[3,128,256]{2,1,0:T(8,128)} copy(f32[3,128,256]{2,1,0:T(8,128)} %get-tuple-element.5) | data formatting | bytes 786432

commit v2 on v1

v2 whole, which is shorter than its diff:
```python
import functools
import itertools
import math

import jax
import jax.numpy as jnp
import ml_dtypes
import numpy as np
from jax import lax
from jax.experimental import pallas as pl
from jax.experimental.pallas import tpu as pltpu
from jax.sharding import PartitionSpec as P

DAMPING = 0.3
STIFFNESS = 0.25
TIME_STEP = 0.25
MESH = pl.DeviceIdType.MESH
F32 = jnp.float32
BF16 = jnp.bfloat16


(T_WA, T_WAQ, T_W1R, T_W1I, T_W2, T_W2I, T_BR, T_BI, T_W3, T_W3Q, T_S2, T_S2I) = (
    0, 1, 2, 3, 4, 5, 6, 7, 8, 9, 10, 13,
)
N_TABLES = 16


def angle(left, right, length):
    product = np.arange(left)[:, None] * np.arange(right)[None, :] % length
    return 2.0 * math.pi * product / length


def matrices():
    out = np.zeros((N_TABLES, 256, 256))
    th = angle(128, 128, 128)
    cos, sin = np.cos(th), np.sin(th)
    out[T_WA] = np.block([[cos, sin], [-sin, cos]])
    scale = -(2.0**-24)
    out[T_W3] = 2.0 * scale * np.block([[cos, sin], [-sin, cos]])
    ph = th + 2.0 * math.pi * np.arange(128)[None, :] / 256.0
    low, high = np.arange(1, 64), np.arange(64, 128)
    sign = 1.0 - 2.0 * (np.arange(128) % 2)
    q = np.zeros((2, 128, 2, 128))
    q[0, 0, 0], q[1, 0, 0] = 1.0, sign
    q[0, low, 0], q[1, low, 0] = cos[low], -sin[low]
    q[0, high, 1], q[1, high, 1] = np.cos(ph)[high], -np.sin(ph)[high]
    out[T_WAQ] = q.reshape(256, 256)
    weight = np.full((128, 1, 1), 2.0)
    weight[0] = 1.0
    out[T_W3Q] = scale * (q * weight).reshape(256, 256)
    th = angle(256, 128, 256)
    cos, sin = np.cos(th), np.sin(th)
    out[T_W1R] = np.concatenate([cos, sin], 1)
    out[T_W1I] = np.concatenate([-sin, cos], 1)
    out[T_BR] = np.concatenate([cos.T, sin.T], 0)
    out[T_BI] = np.concatenate([-sin.T, cos.T], 0)
    th = angle(16, 16, 16)
    cos, sin = np.cos(th), np.sin(th)
    eight = np.eye(8)
    wc = np.einsum("ab,id->aidb", eight, cos).reshape(128, 128)
    ws = np.einsum("ab,id->aidb", eight, sin).reshape(128, 128)
    out[T_W2] = np.block([[wc, -ws], [ws, wc]])
    out[T_W2I] = np.block([[wc.T, ws.T], [-ws.T, wc.T]])
    for m in range(3):
        sc, ss = np.zeros((128, 128)), np.zeros((128, 128))
        for j in range(2):
            rows = slice(48 * j + 16 * m, 48 * j + 16 * m + 16)
            cols = slice(16 * j, 16 * j + 16)
            sc[rows, cols], ss[rows, cols] = cos, sin
        out[T_S2 + m] = np.block([[sc, -ss], [ss, sc]])
        out[T_S2I + m] = np.block([[sc.T, ss.T], [-ss.T, sc.T]])
    return out


def two_parts(value):
    high = value.astype(np.float32).astype(ml_dtypes.bfloat16)
    low = (value - high.astype(np.float64)).astype(np.float32).astype(ml_dtypes.bfloat16)
    return np.stack([high, low])


def twiddles():
    th = 2.0 * math.pi * (np.arange(256)[:, None] * (np.arange(128) % 16)[None, :]) / 4096.0
    ty = angle(16, 128, 4096)
    return np.concatenate([np.cos(th), np.sin(th), np.cos(ty), np.sin(ty)], 0).astype(np.float32)


def split(value):
    high = value.astype(BF16)
    return high, (value - high.astype(F32)).astype(BF16)


def product(a, b, form=(((1,), (0,)), ((), ()))):
    dot = functools.partial(lax.dot_general, dimension_numbers=form, preferred_element_type=F32)
    return dot(a[0], b[0]) + (dot(a[0], b[1]) + dot(a[1], b[0]))


LANES = (((1,), (1,)), ((), ()))


def cross(left, right):
    return [
        left[1] * right[2] - left[2] * right[1],
        left[2] * right[0] - left[0] * right[2],
        left[0] * right[1] - left[1] * right[0],
    ]


def squared(v):
    return v[0] * v[0] + v[1] * v[1] + v[2] * v[2]


def far_first(n_x, n_y, n_z):
    def far(o):
        return sum(min(d, k - d) for d, k in zip(o, (n_x, n_y, n_z)))

    offsets = [o for o in itertools.product(range(n_x), range(n_y), range(n_z), range(2)) if any(o)]
    mixed = np.random.RandomState(1).permutation(len(offsets))
    return sorted((offsets[k] for k in mixed), key=lambda o: -far(o))


def kernel(sizes, mag_h, occ_h, ks_h, cb_h, tw_h, out_ref, mag, occ, ks, cb, tw, m0l, fb, k1, dm, ex,
           mr, hb, kt, kr, kr2, kst, s1, r1, s2, r2, u, zb, xs, ys, pb, os, load_sem, ty_send, ty_recv,
           h_send, h_recv, k_send, k_recv, a_send, a_recv, b_send, b_recv, f_send, f_recv):
    n_x, n_y, n_z = sizes
    n_ty = 2 * n_z
    n = n_x * n_y * n_ty
    tx, ty = lax.axis_index("tx"), lax.axis_index("ty")
    me = tx * n_ty + ty
    px, py, pz, pc = tx // n_y, lax.rem(tx, n_y), ty // 2, lax.rem(ty, 2)
    at_x = [lax.rem(px + d, n_x) * n_y for d in range(n_x)]
    at_y = [lax.rem(py + d, n_y) for d in range(n_y)]
    at_z = [lax.rem(pz + d, n_z) * 2 for d in range(n_z)]
    at_c = [pc, 1 - pc]
    others = far_first(n_x, n_y, n_z)

    loads = [
        pltpu.make_async_copy(mag_h, mag, load_sem.at[0]),
        pltpu.make_async_copy(occ_h, occ, load_sem.at[1]),
        pltpu.make_async_copy(ks_h.at[:, pl.ds(0, 24), :], ks, load_sem.at[2]),
        pltpu.make_async_copy(cb_h, cb, load_sem.at[3]),
        pltpu.make_async_copy(tw_h, tw, load_sem.at[4]),
    ]
    for k in (0, 1, 4, 3, 2):
        loads[k].start()

    barrier = pltpu.get_barrier_semaphore()
    for dx, dy, dz, dc in others:
        to = (at_x[dx] + at_y[dy], at_z[dz] + at_c[dc])
        pl.semaphore_signal(barrier, inc=1, device_id=to, device_id_type=MESH)
    loads[0].wait()
    loads[1].wait()
    occf = occ[...].astype(F32)
    for m in range(3):
        m0l[m] = mag[m] * occf
    pl.semaphore_wait(barrier, n - 1)

    def table(k):
        return cb[0, k], cb[1, k]

    mine = pl.ds(pl.multiple_of(ty * 256, 256), 256)
    own_rows = pl.ds(pl.multiple_of(ty * 16, 16), 16)
    for m in (2, 0, 1):
        for dx, dy, dz, dc in others:
            if dx == 0 and dy == 0:
                to = at_z[dz] + at_c[dc]
                pltpu.make_async_remote_copy(
                    src_ref=m0l.at[m, pl.ds(pl.multiple_of(to * 16, 16), 16), :], dst_ref=fb.at[0, m, :, mine],
                    send_sem=ty_send, recv_sem=ty_recv.at[m], device_id=(tx, to), device_id_type=MESH,
                ).start()
        pltpu.make_async_copy(m0l.at[m, own_rows, :], fb.at[0, m, :, mine], ty_recv.at[m]).start()

    loads[3].wait()
    loads[4].wait()
    own = pl.ds(pl.multiple_of(me * 4, 4), 4)

    def exchange(m, source, target, send, recv):
        for dx, dy, dz, dc in others:
            a, b = at_x[dx] + at_y[dy], at_z[dz] + at_c[dc]
            there = pl.ds(pl.multiple_of((a * n_ty + b) * 4, 4), 4)
            pltpu.make_async_remote_copy(
                src_ref=source.at[m, there, :], dst_ref=target.at[m, own, :],
                send_sem=send, recv_sem=recv.at[m], device_id=(a, b), device_id_type=MESH,
            ).start()
        pltpu.make_async_copy(source.at[m, own, :], target.at[m, own, :], recv.at[m]).start()

    def arrived(m, target, recv):
        pltpu.make_async_copy(target.at[m], target.at[m], recv.at[m]).wait()

    def sent(source, send):
        rest = source.at[:, pl.ds(0, 4 * (n - 1)), :]
        pltpu.make_async_copy(rest, rest, send).wait()

    lane = lax.broadcasted_iota(jnp.int32, (128, 128), 1)
    after, before = lax.rem(me + 1, n), lax.rem(me + n - 1, n)

    def row_copy():
        return pltpu.make_async_remote_copy(
            src_ref=kr, dst_ref=kr2, send_sem=k_send, recv_sem=k_recv, device_id=(0, 0), device_id_type=MESH
        )

    def kernel_tables():
        loads[2].wait()
        upper = me >= n // 2
        top = lax.broadcasted_iota(jnp.int32, (8, 256), 0) == 0
        for k in range(4):
            for d in range(16):
                kr[k, pl.ds(d, 1), :] = ks[k, pl.ds(0, 1), pl.ds(256 * d, 256)]

        @pl.when(me == n // 2)
        def _():
            row_copy().start()

        for k in range(4):
            for h in range(2):
                tiles = []
                for d in range(16):
                    tile = ks[k, pl.ds(8 * h, 8), pl.ds(256 * d, 256)]
                    if h == 0:
                        other = ks[k, pl.ds(16, 8), pl.ds(256 * d, 256)]
                        tile = jnp.where(jnp.logical_and(top, upper), other, tile)
                    tiles.append(tile)
                kt[k, h] = jnp.concatenate(tiles, 0).T

        @pl.when(me == n // 2)
        def _():
            row_copy().wait_send()

        @pl.when(me == 0)
        def _():
            row_copy().wait_recv()
            for k in range(4):
                rows = jnp.concatenate([kr[k], kr2[k], jnp.zeros((96, 256), F32)], 0)
                kst[k] = rows.T

    def step(it, _):
        def y_forward(t, _):
            m = lax.rem(t + 2, 3)

            @pl.when(it == 0)
            def _():
                arrived(m, fb.at[0], ty_recv)

            a = [fb[it, m, :, pl.ds(128 * k, 128)] for k in range(16)]
            real, imag = [None] * 17, [None] * 17
            for c in range(9):
                sums = []
                for odd in range(2):
                    re, im = None, None
                    for k in range(odd, 16, 2):
                        w = 2.0 * math.pi * (c * k % 32) / 32.0
                        wr, wi = round(math.cos(w), 15), round(-math.sin(w), 15)
                        if wr != 0.0:
                            re = a[k] * wr if re is None else re + a[k] * wr
                        if wi != 0.0:
                            im = a[k] * wi if im is None else im + a[k] * wi
                    zero = jnp.zeros_like(a[0])
                    sums.append((zero if re is None else re, zero if im is None else im))
                (er, ei), (ro, io) = sums
                real[c], imag[c] = er + ro, ei + io
                real[16 - c], imag[16 - c] = er - ro, io - ei
            for c in range(16):
                if c == 0:
                    vr, vi = real[0], real[16]
                else:
                    cos, sin = tw[pl.ds(512 + c, 1), :], tw[pl.ds(528 + c, 1), :]
                    vr, vi = real[c] * cos + imag[c] * sin, imag[c] * cos - real[c] * sin
                for part, v in enumerate((vr, vi)):
                    for k, piece in enumerate(split(v)):
                        u[k, pl.ds(16 * c, 16), pl.ds(128 * part, 128)] = piece
            full = product(table(T_WA), (u[0], u[1]), LANES)
            first = product(table(T_WAQ), (u[0, pl.ds(0, 128)], u[1, pl.ds(0, 128)]), LANES)
            for part in range(2):
                rows = slice(128 * part, 128 * part + 128)
                s1[m, pl.ds(2 * part, 128, stride=4), :] = jnp.where(lane < 16, first[rows], full[rows, :128])
                s1[m, pl.ds(2 * part + 1, 128, stride=4), :] = full[rows, 128:]
            exchange(m, s1, r1, a_send, a_recv)
            return 0

        @pl.when(it == 1)
        def _():
            sent(s1, a_send)
            sent(s2, b_send)

        lax.fori_loop(0, 3, y_forward, 0)

        halos = []
        for side, (to, row) in enumerate(((after, 15), (before, 0))):
            halos.append(pltpu.make_async_remote_copy(
                src_ref=fb.at[it, :, row], dst_ref=hb.at[it, side, pl.ds(0, 3)],
                send_sem=h_send.at[side], recv_sem=h_recv.at[it, side],
                device_id=(to // n_ty, lax.rem(to, n_ty)), device_id_type=MESH,
            ))
        for halo in halos:
            halo.start()

        @pl.when(it == 0)
        def _():
            kernel_tables()

        def x_forward(m, _):
            arrived(m, r1, a_recv)
            for part in range(2):
                for h in range(2):
                    block = r1[m, pl.ds(2 * part + h, 128, stride=4), :]
                    for k, piece in enumerate(split(block)):
                        xs[k, pl.ds(128 * part, 128), pl.ds(128 * h, 128)] = piece
            x = (xs[0], xs[1])
            tr, ti = product(table(T_W1R), x), product(table(T_W1I), x)
            cos, sin = tw[pl.ds(0, 256), :], tw[pl.ds(256, 256), :]
            for h in range(2):
                ar, ai = tr[:, 128 * h:128 * h + 128], ti[:, 128 * h:128 * h + 128]
                v = jnp.concatenate([ar * cos + ai * sin, ai * cos - ar * sin], 1)
                z = product(split(v), table(T_W2))
                if isinstance(m, int):
                    zb[m, h, 0] = kt[m, h] * z[:, :128]
                    zb[m, h, 1] = kt[m, h] * z[:, 128:]
                else:
                    zb[m, h, 0] = z[:, :128]
                    zb[m, h, 1] = z[:, 128:]
            return 0

        def mirrored_rows(group):
            cos, sin = tw[pl.ds(0, 256), :], tw[pl.ds(256, 256), :]
            seq = jnp.zeros((128, 128), F32)
            for j in range(2):
                for m in group:
                    block = r1[m, pl.ds(2 * j, 128, stride=4), :]
                    place = 48 * j + 16 * m
                    inside = jnp.logical_and(lane >= place, lane < place + 16)
                    seq = jnp.where(inside, pltpu.roll(block, place, 1) if place else block, seq)
            seq = split(seq)
            ar = product((cb[0, T_W1R][:, :128], cb[1, T_W1R][:, :128]), seq)
            ai = product((cb[0, T_W1I][:, :128], cb[1, T_W1I][:, :128]), seq)
            v = split(jnp.concatenate([ar * cos + ai * sin, ai * cos - ar * sin], 1))
            z = [product(v, table(T_S2 + m)) for m in group]
            two = lambda k: jnp.concatenate([kst[k], kst[k]], 1)
            if len(group) == 1:
                field = [two(2) * z[0]]
            else:
                xx, yy, xy = two(0), two(1), two(3)
                field = [xx * z[0] + xy * z[1], xy * z[0] + yy * z[1]]
            back = 0.0
            for m, f in zip(group, field):
                back = back + product(split(f), table(T_S2I + m))
            br, bi = back[:, :128], back[:, 128:]
            yr, yi = split(br * cos - bi * sin), split(bi * cos + br * sin)
            os[...] = product((cb[0, T_BR][:128], cb[1, T_BR][:128]), yr) + product(
                (cb[0, T_BI][:128], cb[1, T_BI][:128]), yi)

        def gains(k, _):
            h, part = k // 2, lax.rem(k, 2)
            x, y = zb[0, h, part], zb[1, h, part]
            xy = kt[3, h]
            zb[0, h, part] = kt[0, h] * x + xy * y
            zb[1, h, part] = xy * x + kt[1, h] * y
            return 0

        def x_inverse(m, _):
            cos, sin = tw[pl.ds(0, 256), :], tw[pl.ds(256, 256), :]
            for h in range(2):
                field = split(jnp.concatenate([zb[m, h, 0], zb[m, h, 1]], 1))
                p = product(field, table(T_W2I))
                pr, pi = p[:, :128], p[:, 128:]
                for part, v in enumerate((pr * cos - pi * sin, pi * cos + pr * sin)):
                    for k, piece in enumerate(split(v)):
                        ys[k, part, :, pl.ds(128 * h, 128)] = piece
            o = product(table(T_BR), (ys[0, 0], ys[1, 0])) + product(table(T_BI), (ys[0, 1], ys[1, 1]))
            for part in range(2):
                for h in range(2):
                    s2[m, pl.ds(2 * part + h, 128, stride=4), :] = (
                        o[128 * part:128 * part + 128, 128 * h:128 * h + 128])

            @pl.when(me == 0)
            def _():
                for j in range(2):
                    place = pl.ds(2 * j, 128, stride=4)
                    moved = pltpu.roll(os[...], 128 - 48 * j - 16 * m, 1)
                    s2[m, place, :] = jnp.where(lane < 16, moved, s2[m, place, :])

            exchange(m, s2, r2, b_send, b_recv)
            return 0

        x_forward(2, 0)

        @pl.when(me == 0)
        def _():
            mirrored_rows((2,))

        x_inverse(2, 0)
        lax.fori_loop(0, 2, x_forward, 0)

        @pl.when(me == 0)
        def _():
            mirrored_rows((0, 1))

        lax.fori_loop(0, 4, gains, 0)
        lax.fori_loop(0, 2, x_inverse, 0)

        for halo in halos:
            halo.wait_recv()
        row = lax.broadcasted_iota(jnp.int32, (16, 2048), 0)
        col = lax.broadcasted_iota(jnp.int32, (16, 2048), 1)
        for m in range(3):
            f = fb[it, m]
            low = jnp.where(me > 0, hb[it, 0, pl.ds(m, 1), :], 0.0)
            high = jnp.where(me < n - 1, hb[it, 1, pl.ds(m, 1), :], 0.0)
            up = jnp.where(row == 0, low, pltpu.roll(f, 1, 0))
            down = jnp.where(row == 15, high, pltpu.roll(f, 15, 0))
            left = jnp.where(col == 0, 0.0, pltpu.roll(f, 1, 1))
            right = jnp.where(col == 2047, 0.0, pltpu.roll(f, 2047, 1))
            ex[m] = STIFFNESS * (down + up + right + left)
        for halo in halos:
            halo.wait_send()

        def y_inverse(t, _):
            m = lax.rem(t + 2, 3)
            arrived(m, r2, b_recv)
            for part in range(2):
                for h in range(2):
                    block = r2[m, pl.ds(2 * part + h, 128, stride=4), :].T
                    for k, piece in enumerate(split(block)):
                        xs[k, pl.ds(128 * h, 128), pl.ds(128 * part, 128)] = piece
            pb[...] = product((xs[0], xs[1]), table(T_W3))
            pq = product((xs[0, pl.ds(0, 16), :], xs[1, pl.ds(0, 16), :]), table(T_W3Q))
            real, imag = [None] * 16, [None] * 16
            for c in range(1, 16):
                cos, sin = tw[pl.ds(512 + c, 1), :], tw[pl.ds(528 + c, 1), :]
                br, bi = pb[pl.ds(16 * c, 16), pl.ds(0, 128)], pb[pl.ds(16 * c, 16), pl.ds(128, 128)]
                real[c], imag[c] = br * cos - bi * sin, bi * cos + br * sin
            ends = (pq[:, :128] + pq[:, 128:], pq[:, :128] - pq[:, 128:])
            pairs = []
            for odd in range(2):
                pairs.append([
                    (real[c] - real[16 - c], imag[c] + imag[16 - c]) if odd
                    else (real[c] + real[16 - c], imag[c] - imag[16 - c]) for c in range(1, 8)
                ])
            for a in range(16):
                total = ends[a % 2]
                for c in range(1, 9):
                    re, im = pairs[a % 2][c - 1] if c < 8 else (real[8], imag[8])
                    w = 2.0 * math.pi * (c * a % 32) / 32.0
                    wr, wi = round(math.cos(w), 15), round(math.sin(w), 15)
                    if wr != 0.0:
                        total = total + re * wr
                    if wi != 0.0:
                        total = total - im * wi
                dm[m, :, pl.ds(128 * a, 128)] = total
            return 0

        lax.fori_loop(0, 3, y_inverse, 0)

        def advance(j, _):
            far = j // 2
            dz = jnp.where(far == 0, 2, jnp.where(far == 1, 1, jnp.where(far == 2, 3, 0)))
            to = lax.rem(pz + dz, n_z) * 2 + lax.rem(pc + j + 1, 2)
            cols = pl.ds(pl.multiple_of(to * 256, 256), 256)
            m0 = [fb[0, m, :, cols] for m in range(3)]
            f = [fb[it, m, :, cols] for m in range(3)]
            heff = [dm[m, :, cols] + ex[m, :, cols] for m in range(3)]
            torque = cross(f, heff)
            damped = cross(f, torque)
            rate = [(t + DAMPING * d) * (-1.0 / (1.0 + DAMPING * DAMPING)) for t, d in zip(torque, damped)]

            @pl.when(it == 0)
            def _():
                filled = jnp.where(squared(m0) > 0.5, 0.0, 1.0)
                v = [m + TIME_STEP * r for m, r in zip(m0, rate)]
                root = jnp.sqrt(squared(v) + filled)
                for m in range(3):
                    k1[m, :, cols] = rate[m]
                    fb[1, m, :, cols] = v[m] / root

            @pl.when(it == 1)
            def _():
                along = rate[0] * m0[0] + rate[1] * m0[1] + rate[2] * m0[2]
                for m in range(3):
                    mr[m, :, cols] = k1[m, :, cols] + (rate[m] - along * m0[m])

                @pl.when(j < n_ty - 1)
                def _():
                    pltpu.make_async_remote_copy(
                        src_ref=mr.at[:, :, cols], dst_ref=out_ref.at[:, own_rows, :],
                        send_sem=f_send, recv_sem=f_recv, device_id=(tx, to), device_id_type=MESH,
                    ).start()

                @pl.when(j == n_ty - 1)
                def _():
                    pltpu.make_async_copy(mr.at[:, :, cols], out_ref.at[:, own_rows, :], f_recv).start()

            return 0

        lax.fori_loop(0, n_ty, advance, 0)
        return 0

    lax.fori_loop(0, 2, step, 0)
    rest = m0l.at[:, pl.ds(0, 16 * (n_ty - 1)), :]
    pltpu.make_async_copy(rest, rest, ty_send).wait()
    sent(s1, a_send)
    sent(s2, b_send)
    pltpu.make_async_copy(out_ref, out_ref, f_recv).wait()
    pltpu.make_async_copy(rest, rest, f_send).wait()


def body(sizes, mag, occupancy, kernel_spectrum):
    cb = jnp.asarray(two_parts(matrices()))
    tw = jnp.asarray(twiddles())
    V = pltpu.VMEM
    D = pltpu.SemaphoreType.DMA
    block = (3, 128, 256)
    band = (3, 16, 2048)
    slots = (3, 512, 128)
    doubled = pl.pallas_call(
        functools.partial(kernel, sizes),
        out_shape=jax.ShapeDtypeStruct(block, F32),
        in_specs=[pl.BlockSpec(memory_space=pl.ANY)] * 5,
        out_specs=pl.BlockSpec(memory_space=pltpu.VMEM),
        scratch_shapes=[
            V(block, F32), V((128, 256), jnp.int32), V((4, 24, 4096), F32), V((2, N_TABLES, 256, 256), BF16),
            V((544, 128), F32),
            V(block, F32), V((2,) + band, F32), V(band, F32), V(band, F32), V(band, F32),
            V(band, F32), V((2, 2, 8, 2048), F32), V((4, 2, 256, 128), F32),
            V((4, 16, 256), F32), V((4, 16, 256), F32), V((4, 256, 128), F32),
            V(slots, F32), V(slots, F32), V(slots, F32), V(slots, F32),
            V((2, 256, 256), BF16), V((3, 2, 2, 256, 128), F32),
            V((2, 256, 256), BF16), V((2, 2, 256, 256), BF16), V((256, 256), F32), V((128, 128), F32),
            D((5,)), D, D((3,)), D((2,)), D((2, 2)), D, D, D, D((3,)), D, D((3,)), D, D,
        ],
        compiler_params=pltpu.CompilerParams(
            collective_id=0, has_side_effects=True, vmem_limit_bytes=56 * 1024 * 1024
        ),
    )(mag, occupancy, kernel_spectrum, cb, tw)
    occ = occupancy.astype(F32)
    mean_rate = 0.5 * doubled
    v = mag * occ[None] + TIME_STEP * mean_rate
    root = jnp.sqrt(jnp.sum(v * v, axis=0) + 1.0 - occ)
    return v / root[None], mean_rate


def solution(mesh):
    n_tx, n_ty = mesh.shape["tx"], mesh.shape["ty"]
    side = math.isqrt(n_tx)
    return jax.shard_map(
        functools.partial(body, (side, side, n_ty // 2)),
        mesh=mesh,
        in_specs=(P(None, "tx", "ty"), P("tx", "ty"), P(None, ("tx", "ty"), None)),
        out_specs=(P(None, "tx", "ty"), P(None, "tx", "ty")),
        check_vma=False,
    )
```

time: 104 us -> 80.2 us (0.77)
  Pallas kernels: 99.7 us -> 75.2 us
  other arithmetic: 0 us -> 4.06 us
  local copies, waits for them, and re-layouts: 3.53 us -> 0.01 us
    pallas_call x1, Pallas kernels: 99.7 us -> 75.2 us  [body(): pl.pallas_call(functools.partial(kernel, sizes), out_shape=jax.ShapeDtype...]
    unnamed x2 -> x4, local copies, waits for them, and re-layouts: 3.53 us -> 0.01 us
    mul x0 -> x1, other arithmetic: none -> 1.97 us  [body(): mean_rate = 0.5 * doubled]
    reduce_sum x0 -> x1, other arithmetic: none -> 1.08 us  [body(): root = jnp.sqrt(jnp.sum(v * v, axis=0) + 1.0 - occ)]
where the time goes in v2:
time: 80.2 us; the launch traced here: 80 us
  Pallas kernels  75.2 us (94%)
  other arithmetic  4.06 us (5%)
    pallas_call x1, Pallas kernels, body(): pl.pallas_call(functools.partial(kernel, sizes), out_shape=jax.ShapeDtype...  75.2 us
    mul x1, other arithmetic, body(): mean_rate = 0.5 * doubled  1.97 us

profile of v2, /device:TPU:1, one launch (start us, length us, event | category | flops | bytes accessed | tf_op | source)
XLA Modules:
  0.0 80.0 jit_solution(18070260447629828949)
XLA Ops:
  0.6 0.0 copy-start
  0.6 1.0 %convert_element_type.3 = f32[128,256]{1,0:T(8,128)S(1)} convert(s32[128,256]{1,0:T(8,128)} %occ_h.1) | non-fusion elementwise | flops 32768 | bytes 262144 | tf_op jit(solution)/shard_map/convert_element_type | solution.py:532
  1.6 0.0 copy-start.1
  1.6 75.2 %shard_map.68 = f32[3,128,256]{2,1,0:T(8,128)} custom-call(f32[3,128,256]{2,1,0:T(8,128)} %mag_h.1, s32[128,256]{1,0:T(8,128)} %occ_h.1, f32[4,32,4096]{2,1,0:T(8,128)} %ks_h.1, bf16[2,16,256,256]{3,2,1,0:T(8,128)(2,1)} %constant.13.clone.cb_h, f32[544,128]{1,0:T(8,128)} %constant.14.clone.tw_h), custom_call_target="tpu_custom_call" | custom-call | tf_op jit(solution)/shard_map/pallas_call | solution.py:512
  76.8 0.0 copy-done
  76.9 1.1 %multiply_reduce_fusion = f32[128,256]{1,0:T(8,128)S(1)} fusion(f32[3,128,256]{2,1,0:T(8,128)} %shard_map.68, f32[3,128,256]{2,1,0:T(8,128)S(1)} %copy-done, f32[128,256]{1,0:T(8,128)S(1)} %convert_element_type.3), kind=kLoop, calls=%fused_computation | loop fusion | flops 458752 | bytes 1048576 | tf_op jit(solution)/shard_map/reduce_sum | solution.py:535
  77.9 0.0 copy-done.1
  78.0 2.0 %broadcast_multiply_fusion = (f32[3,128,256]{2,1,0:T(8,128)}, f32[3,128,256]{2,1,0:T(8,128)}) fusion(f32[3,128,256]{2,1,0:T(8,128)} %shard_map.68, f32[128,256]{1,0:T(8,128)S(1)} %subtract_sqrt_fusion, f32[3,128,256]{2,1,0:T(8,128)S(1)} %copy-done, f32[128,256]{1,0:T(8,128)S(1)} %convert_element_type.3), kind=kLoop, calls=%fused_computation.2 | loop fusion | flops 491520 | bytes 1835008 | tf_op jit(solution)/shard_map/mul | solution.py:533
  (1 shorter events, 0.0 us)
Async XLA Ops:
  0.6 76.2 %copy-start = (f32[3,128,256]{2,1,0:T(8,128)S(1)}, f32[3,128,256]{2,1,0:T(8,128)}, u32[]{:S(2)}) copy-start(f32[3,128,256]{2,1,0:T(8,128)} %mag_h.1) | copy-start | bytes 1179652
  1.6 76.3 %copy-start.1 = (s32[128,256]{1,0:T(8,128)S(1)}, s32[128,256]{1,0:T(8,128)}, u32[]{:S(2)}) copy-start(s32[128,256]{1,0:T(8,128)} %occ_h.1) | copy-start | bytes 393220

commit v3 on v2

--- a/solution.py
+++ b/solution.py
@@ -119,8 +119,8 @@
 
 
 def kernel(sizes, mag_h, occ_h, ks_h, cb_h, tw_h, out_ref, mag, occ, ks, cb, tw, m0l, fb, k1, dm, ex,
-           mr, hb, kt, kr, kr2, kst, s1, r1, s2, r2, u, zb, xs, ys, pb, os, load_sem, ty_send, ty_recv,
-           h_send, h_recv, k_send, k_recv, a_send, a_recv, b_send, b_recv, f_send, f_recv):
+           mr, hb, kt, kr, kr2, kst, s1, r1, s2, r2, u, zb, xs, ys, pb, pq, os, load_sem, ty_send, ty_recv,
+           h_send, h_recv, k_send, k_recv, a_send, a_recv, b_send, b_recv, f_send, f_recv, ready):
     n_x, n_y, n_z = sizes
     n_ty = 2 * n_z
     n = n_x * n_y * n_ty
@@ -144,7 +144,9 @@
         loads[k].start()
 
     barrier = pltpu.get_barrier_semaphore()
-    for dx, dy, dz, dc in others:
+    line = [o for o in others if o[:2] == (0, 0)]
+    plane = [o for o in others if o[2:] == (0, 0)]
+    for dx, dy, dz, dc in plane + line:
         to = (at_x[dx] + at_y[dy], at_z[dz] + at_c[dc])
         pl.semaphore_signal(barrier, inc=1, device_id=to, device_id_type=MESH)
     loads[0].wait()
@@ -152,7 +154,7 @@
     occf = occ[...].astype(F32)
     for m in range(3):
         m0l[m] = mag[m] * occf
-    pl.semaphore_wait(barrier, n - 1)
+    pl.semaphore_wait(barrier, len(plane) + len(line))
 
     def table(k):
         return cb[0, k], cb[1, k]
@@ -160,17 +162,19 @@
     mine = pl.ds(pl.multiple_of(ty * 256, 256), 256)
     own_rows = pl.ds(pl.multiple_of(ty * 16, 16), 16)
     for m in (2, 0, 1):
-        for dx, dy, dz, dc in others:
-            if dx == 0 and dy == 0:
-                to = at_z[dz] + at_c[dc]
-                pltpu.make_async_remote_copy(
-                    src_ref=m0l.at[m, pl.ds(pl.multiple_of(to * 16, 16), 16), :], dst_ref=fb.at[0, m, :, mine],
-                    send_sem=ty_send, recv_sem=ty_recv.at[m], device_id=(tx, to), device_id_type=MESH,
-                ).start()
+        for _, _, dz, dc in line:
+            to = at_z[dz] + at_c[dc]
+            pltpu.make_async_remote_copy(
+                src_ref=m0l.at[m, pl.ds(pl.multiple_of(to * 16, 16), 16), :], dst_ref=fb.at[0, m, :, mine],
+                send_sem=ty_send, recv_sem=ty_recv.at[m], device_id=(tx, to), device_id_type=MESH,
+            ).start()
         pltpu.make_async_copy(m0l.at[m, own_rows, :], fb.at[0, m, :, mine], ty_recv.at[m]).start()
 
+    for _, _, dz, dc in line:
+        pl.semaphore_signal(ready, inc=1, device_id=(tx, at_z[dz] + at_c[dc]), device_id_type=MESH)
     loads[3].wait()
     loads[4].wait()
+    pl.semaphore_wait(ready, len(line))
     own = pl.ds(pl.multiple_of(me * 4, 4), 4)
 
     def exchange(m, source, target, send, recv):
@@ -233,9 +237,12 @@
                 kst[k] = rows.T
 
     def step(it, _):
-        def y_forward(t, _):
-            m = lax.rem(t + 2, 3)
-
+        def place(m, c):
+            if isinstance(m, int) and m == 2:
+                return 0, 16 * c
+            return 1 + c // 8, pl.multiple_of(128 * m + 16 * (c % 8), 16)
+
+        def y_first(m, _):
             @pl.when(it == 0)
             def _():
                 arrived(m, fb.at[0], ty_recv)
@@ -264,16 +271,21 @@
                 else:
                     cos, sin = tw[pl.ds(512 + c, 1), :], tw[pl.ds(528 + c, 1), :]
                     vr, vi = real[c] * cos + imag[c] * sin, imag[c] * cos - real[c] * sin
+                chunk, start = place(m, c)
                 for part, v in enumerate((vr, vi)):
                     for k, piece in enumerate(split(v)):
-                        u[k, pl.ds(16 * c, 16), pl.ds(128 * part, 128)] = piece
-            full = product(table(T_WA), (u[0], u[1]), LANES)
-            first = product(table(T_WAQ), (u[0, pl.ds(0, 128)], u[1, pl.ds(0, 128)]), LANES)
+                        u[k, chunk, pl.ds(start, 16), pl.ds(128 * part, 128)] = piece
+            return 0
+
+        def y_second(g, _):
+            full = product(table(T_WA), (u[0, g], u[1, g]), LANES)
+            first = product(table(T_WAQ), (u[0, g], u[1, g]), LANES)
             for part in range(2):
-                rows = slice(128 * part, 128 * part + 128)
-                s1[m, pl.ds(2 * part, 128, stride=4), :] = jnp.where(lane < 16, first[rows], full[rows, :128])
-                s1[m, pl.ds(2 * part + 1, 128, stride=4), :] = full[rows, 128:]
-            exchange(m, s1, r1, a_send, a_recv)
+                for b in range(2):
+                    block = (slice(128 * part, 128 * part + 128), slice(128 * b, 128 * b + 128))
+                    inside = jnp.logical_and(lane < 16, g == 1 if b else g < 2)
+                    s1[g, pl.ds(2 * part + b, 128, stride=4), :] = jnp.where(inside, first[block], full[block])
+            exchange(g, s1, r1, a_send, a_recv)
             return 0
 
         @pl.when(it == 1)
@@ -281,7 +293,10 @@
             sent(s1, a_send)
             sent(s2, b_send)
 
-        lax.fori_loop(0, 3, y_forward, 0)
+        y_first(2, 0)
+        y_second(0, 0)
+        lax.fori_loop(0, 2, y_first, 0)
+        lax.fori_loop(1, 3, y_second, 0)
 
         halos = []
         for side, (to, row) in enumerate(((after, 15), (before, 0))):
@@ -297,37 +312,15 @@
         def _():
             kernel_tables()
 
-        def x_forward(m, _):
-            arrived(m, r1, a_recv)
-            for part in range(2):
-                for h in range(2):
-                    block = r1[m, pl.ds(2 * part + h, 128, stride=4), :]
-                    for k, piece in enumerate(split(block)):
-                        xs[k, pl.ds(128 * part, 128), pl.ds(128 * h, 128)] = piece
-            x = (xs[0], xs[1])
-            tr, ti = product(table(T_W1R), x), product(table(T_W1I), x)
-            cos, sin = tw[pl.ds(0, 256), :], tw[pl.ds(256, 256), :]
-            for h in range(2):
-                ar, ai = tr[:, 128 * h:128 * h + 128], ti[:, 128 * h:128 * h + 128]
-                v = jnp.concatenate([ar * cos + ai * sin, ai * cos - ar * sin], 1)
-                z = product(split(v), table(T_W2))
-                if isinstance(m, int):
-                    zb[m, h, 0] = kt[m, h] * z[:, :128]
-                    zb[m, h, 1] = kt[m, h] * z[:, 128:]
-                else:
-                    zb[m, h, 0] = z[:, :128]
-                    zb[m, h, 1] = z[:, 128:]
-            return 0
-
-        def mirrored_rows(group):
+        def mirrored_rows(g, group):
             cos, sin = tw[pl.ds(0, 256), :], tw[pl.ds(256, 256), :]
             seq = jnp.zeros((128, 128), F32)
             for j in range(2):
-                for m in group:
-                    block = r1[m, pl.ds(2 * j, 128, stride=4), :]
-                    place = 48 * j + 16 * m
-                    inside = jnp.logical_and(lane >= place, lane < place + 16)
-                    seq = jnp.where(inside, pltpu.roll(block, place, 1) if place else block, seq)
+                for b, m in enumerate(group):
+                    block = r1[g, pl.ds(2 * j + b, 128, stride=4), :]
+                    at = 48 * j + 16 * m
+                    inside = jnp.logical_and(lane >= at, lane < at + 16)
+                    seq = jnp.where(inside, pltpu.roll(block, at, 1) if at else block, seq)
             seq = split(seq)
             ar = product((cb[0, T_W1R][:, :128], cb[1, T_W1R][:, :128]), seq)
             ai = product((cb[0, T_W1I][:, :128], cb[1, T_W1I][:, :128]), seq)
@@ -347,54 +340,63 @@
             os[...] = product((cb[0, T_BR][:128], cb[1, T_BR][:128]), yr) + product(
                 (cb[0, T_BI][:128], cb[1, T_BI][:128]), yi)
 
-        def gains(k, _):
-            h, part = k // 2, lax.rem(k, 2)
-            x, y = zb[0, h, part], zb[1, h, part]
-            xy = kt[3, h]
-            zb[0, h, part] = kt[0, h] * x + xy * y
-            zb[1, h, part] = xy * x + kt[1, h] * y
-            return 0
-
-        def x_inverse(m, _):
+        def x_chunk(g, group):
+            arrived(g, r1, a_recv)
+            for part in range(2):
+                for b in range(2):
+                    block = r1[g, pl.ds(2 * part + b, 128, stride=4), :]
+                    for k, piece in enumerate(split(block)):
+                        xs[k, pl.ds(128 * part, 128), pl.ds(128 * b, 128)] = piece
+            x = (xs[0], xs[1])
+            tr, ti = product(table(T_W1R), x), product(table(T_W1I), x)
             cos, sin = tw[pl.ds(0, 256), :], tw[pl.ds(256, 256), :]
-            for h in range(2):
-                field = split(jnp.concatenate([zb[m, h, 0], zb[m, h, 1]], 1))
-                p = product(field, table(T_W2I))
+            for b in range(2):
+                ar, ai = tr[:, 128 * b:128 * b + 128], ti[:, 128 * b:128 * b + 128]
+                v = jnp.concatenate([ar * cos + ai * sin, ai * cos - ar * sin], 1)
+                zb[b] = product(split(v), table(T_W2))
+
+            mirrored = me == 0 if len(group) == 1 else jnp.logical_and(me == 0, g == 1)
+
+            @pl.when(mirrored)
+            def _():
+                mirrored_rows(g, group)
+
+            for b in range(2):
+                pieces = []
+                for part in range(2):
+                    cols = pl.ds(128 * part, 128)
+                    if len(group) == 1:
+                        pieces.append(kt[2, b] * zb[b, :, cols])
+                    else:
+                        pieces.append(kt[b, g - 1] * zb[b, :, cols] + kt[3, g - 1] * zb[1 - b, :, cols])
+                p = product(split(jnp.concatenate(pieces, 1)), table(T_W2I))
                 pr, pi = p[:, :128], p[:, 128:]
                 for part, v in enumerate((pr * cos - pi * sin, pi * cos + pr * sin)):
                     for k, piece in enumerate(split(v)):
-                        ys[k, part, :, pl.ds(128 * h, 128)] = piece
+                        ys[k, part, :, pl.ds(128 * b, 128)] = piece
             o = product(table(T_BR), (ys[0, 0], ys[1, 0])) + product(table(T_BI), (ys[0, 1], ys[1, 1]))
             for part in range(2):
-                for h in range(2):
-                    s2[m, pl.ds(2 * part + h, 128, stride=4), :] = (
-                        o[128 * part:128 * part + 128, 128 * h:128 * h + 128])
-
-            @pl.when(me == 0)
+                for b in range(2):
+                    s2[g, pl.ds(2 * part + b, 128, stride=4), :] = (
+                        o[128 * part:128 * part + 128, 128 * b:128 * b + 128])
+
+            @pl.when(mirrored)
             def _():
                 for j in range(2):
-                    place = pl.ds(2 * j, 128, stride=4)
-                    moved = pltpu.roll(os[...], 128 - 48 * j - 16 * m, 1)
-                    s2[m, place, :] = jnp.where(lane < 16, moved, s2[m, place, :])
-
-            exchange(m, s2, r2, b_send, b_recv)
+                    for b, m in enumerate(group):
+                        rows = pl.ds(2 * j + b, 128, stride=4)
+                        shift = (128 - 48 * j - 16 * m) % 128
+                        moved = pltpu.roll(os[...], shift, 1) if shift else os[...]
+                        s2[g, rows, :] = jnp.where(lane < 16, moved, s2[g, rows, :])
+
+            exchange(g, s2, r2, b_send, b_recv)
+
+        def xy_chunk(g, _):
+            x_chunk(g, (0, 1))
             return 0
 
-        x_forward(2, 0)
-
-        @pl.when(me == 0)
-        def _():
-            mirrored_rows((2,))
-
-        x_inverse(2, 0)
-        lax.fori_loop(0, 2, x_forward, 0)
-
-        @pl.when(me == 0)
-        def _():
-            mirrored_rows((0, 1))
-
-        lax.fori_loop(0, 4, gains, 0)
-        lax.fori_loop(0, 2, x_inverse, 0)
+        x_chunk(0, (2,))
+        lax.fori_loop(1, 3, xy_chunk, 0)
 
         for halo in halos:
             halo.wait_recv()
@@ -412,22 +414,38 @@
         for halo in halos:
             halo.wait_send()
 
-        def y_inverse(t, _):
-            m = lax.rem(t + 2, 3)
-            arrived(m, r2, b_recv)
+        def y_inverse_first(g, _):
+            arrived(g, r2, b_recv)
             for part in range(2):
-                for h in range(2):
-                    block = r2[m, pl.ds(2 * part + h, 128, stride=4), :].T
+                for b in range(2):
+                    block = r2[g, pl.ds(2 * part + b, 128, stride=4), :].T
                     for k, piece in enumerate(split(block)):
-                        xs[k, pl.ds(128 * h, 128), pl.ds(128 * part, 128)] = piece
-            pb[...] = product((xs[0], xs[1]), table(T_W3))
-            pq = product((xs[0, pl.ds(0, 16), :], xs[1, pl.ds(0, 16), :]), table(T_W3Q))
+                        xs[k, pl.ds(128 * b, 128), pl.ds(128 * part, 128)] = piece
+            pb[g] = product((xs[0], xs[1]), table(T_W3))
+
+            def ends(m, row):
+                rows = pl.ds(row, 16)
+                pq[m] = product((xs[0, rows, :], xs[1, rows, :]), table(T_W3Q))
+
+            if isinstance(g, int):
+                ends(2, 0)
+            else:
+                @pl.when(g == 1)
+                def _():
+                    ends(0, 0)
+                    ends(1, 128)
+
+            return 0
+
+        def y_inverse_second(m, _):
             real, imag = [None] * 16, [None] * 16
             for c in range(1, 16):
                 cos, sin = tw[pl.ds(512 + c, 1), :], tw[pl.ds(528 + c, 1), :]
-                br, bi = pb[pl.ds(16 * c, 16), pl.ds(0, 128)], pb[pl.ds(16 * c, 16), pl.ds(128, 128)]
+                chunk, start = place(m, c)
+                br, bi = pb[chunk, pl.ds(start, 16), pl.ds(0, 128)], pb[chunk, pl.ds(start, 16), pl.ds(128, 128)]
                 real[c], imag[c] = br * cos - bi * sin, bi * cos + br * sin
-            ends = (pq[:, :128] + pq[:, 128:], pq[:, :128] - pq[:, 128:])
+            even, odd_part = pq[m, :, pl.ds(0, 128)], pq[m, :, pl.ds(128, 128)]
+            ends = (even + odd_part, even - odd_part)
             pairs = []
             for odd in range(2):
                 pairs.append([
@@ -447,7 +465,10 @@
                 dm[m, :, pl.ds(128 * a, 128)] = total
             return 0
 
-        lax.fori_loop(0, 3, y_inverse, 0)
+        y_inverse_first(0, 0)
+        y_inverse_second(2, 0)
+        lax.fori_loop(1, 3, y_inverse_first, 0)
+        lax.fori_loop(0, 2, y_inverse_second, 0)
 
         def advance(j, _):
             far = j // 2
@@ -521,19 +542,21 @@
             V(band, F32), V((2, 2, 8, 2048), F32), V((4, 2, 256, 128), F32),
             V((4, 16, 256), F32), V((4, 16, 256), F32), V((4, 256, 128), F32),
             V(slots, F32), V(slots, F32), V(slots, F32), V(slots, F32),
-            V((2, 256, 256), BF16), V((3, 2, 2, 256, 128), F32),
-            V((2, 256, 256), BF16), V((2, 2, 256, 256), BF16), V((256, 256), F32), V((128, 128), F32),
+            V((2, 3, 256, 256), BF16), V((2, 256, 256), F32), V((2, 256, 256), BF16), V((2, 2, 256, 256), BF16),
+            V((3, 256, 256), F32), V((3, 16, 256), F32), V((128, 128), F32),
             D((5,)), D, D((3,)), D((2,)), D((2, 2)), D, D, D, D((3,)), D, D((3,)), D, D,
+            pltpu.SemaphoreType.REGULAR,
         ],
         compiler_params=pltpu.CompilerParams(
             collective_id=0, has_side_effects=True, vmem_limit_bytes=56 * 1024 * 1024
         ),
     )(mag, occupancy, kernel_spectrum, cb, tw)
-    occ = occupancy.astype(F32)
+    late, doubled = lax.optimization_barrier((occupancy, doubled))
+    occ = late.astype(F32)
     mean_rate = 0.5 * doubled
-    v = mag * occ[None] + TIME_STEP * mean_rate
-    root = jnp.sqrt(jnp.sum(v * v, axis=0) + 1.0 - occ)
-    return v / root[None], mean_rate
+    v = [mag[m] * occ + TIME_STEP * mean_rate[m] for m in range(3)]
+    root = jnp.sqrt(squared(v) + 1.0 - occ)
+    return jnp.stack([c / root for c in v]), mean_rate
 
 
 def solution(mesh):

time: 80.2 us -> 76.1 us (0.949)
  other arithmetic: 4.06 us -> 1.98 us
  Pallas kernels: 75.2 us -> 73.2 us
    pallas_call x1, Pallas kernels: 75.2 us -> 73.2 us  [body(): pl.pallas_call(functools.partial(kernel, sizes), out_shape=jax.ShapeDtype...]
    reduce_sum x1 -> x0, other arithmetic: 1.08 us -> none  [body(): root = jnp.sqrt(jnp.sum(v * v, axis=0) + 1.0 - occ)]
    convert_element_type x1 -> x0, other arithmetic: 0.97 us -> none  [body(): occ = occupancy.astype(F32)]
    another operation x0 -> x3, other arithmetic: none -> 0.96 us  [body(): return (jnp.stack([c / root for c in v]), mean_rate)]
    mul x1, other arithmetic: 1.97 us -> 1.02 us  [body(): mean_rate = 0.5 * doubled]
where the time goes in v3:
time: 76.1 us; the launch traced here: 75.9 us
  Pallas kernels  73.2 us (96%)
  other arithmetic  1.98 us (3%)
    pallas_call x1, Pallas kernels, body(): pl.pallas_call(functools.partial(kernel, sizes), out_shape=jax.ShapeDtype...  73.2 us

profile of v3, /device:TPU:1, one launch (start us, length us, event | category | flops | bytes accessed | tf_op | source)
XLA Modules:
  0.0 75.9 jit_solution(15577901704630856843)
XLA Ops:
  0.6 0.0 copy-start
  0.6 0.0 copy-start.2
  0.6 73.2 %shard_map.68 = f32[3,128,256]{2,1,0:T(8,128)} custom-call(f32[3,128,256]{2,1,0:T(8,128)} %mag_h.1, s32[128,256]{1,0:T(8,128)} %occ_h.1, f32[4,32,4096]{2,1,0:T(8,128)} %ks_h.1, bf16[2,16,256,256]{3,2,1,0:T(8,128)(2,1)} %constant.10.clone.cb_h, f32[544,128]{1,0:T(8,128)} %constant.11.clone.tw_h), custom_call_target="tpu_custom_call" | custom-call | tf_op jit(solution)/shard_map/pallas_call | solution.py:533
  73.9 1.0 %broadcast_multiply_fusion = f32[3,128,256]{2,1,0:T(8,128)S(1)} fusion(f32[3,128,256]{2,1,0:T(8,128)} %shard_map.68), kind=kLoop, calls=%fused_computation.1 | loop fusion | flops 98304 | bytes 786432 | tf_op jit(solution)/shard_map/mul | solution.py:556
  74.9 0.0 copy-done
  74.9 0.0 copy-done.2
  74.9 0.0 copy-start.1
  74.9 0.1 divide_bitcast_fusion.2
  75.1 0.1 divide_bitcast_fusion.1
  75.1 0.8 %pad_maximum_fusion = f32[3,128,256]{2,1,0:T(8,128)} fusion(f32[1,128,256]{2,1,0:T(8,128)S(1)} %get-tuple-element.9, f32[1,128,256]{2,1,0:T(8,128)S(1)} %get-tuple-element.8, f32[1,128,256]{2,1,0:T(8,128)S(1)} %get-tuple-element.6), kind=kLoop, calls=%fused_computation | loop fusion | flops 196608 | bytes 786432 | tf_op jit(solution)/shard_map/stack | solution.py:559
  75.9 0.0 copy-done.1
Async XLA Ops:
  0.6 74.3 %copy-start = (f32[3,128,256]{2,1,0:T(8,128)S(1)}, f32[3,128,256]{2,1,0:T(8,128)}, u32[]{:S(2)}) copy-start(f32[3,128,256]{2,1,0:T(8,128)} %mag_h.1) | copy-start | bytes 1179652
  0.6 74.3 %copy-start.2 = (s32[128,256]{1,0:T(8,128)S(1)}, s32[128,256]{1,0:T(8,128)}, u32[]{:S(2)}) copy-start(s32[128,256]{1,0:T(8,128)} %occ_h.1) | copy-start | bytes 393220
  74.9 1.0 %copy-start.1 = (f32[3,128,256]{2,1,0:T(8,128)}, f32[3,128,256]{2,1,0:T(8,128)S(1)}, u32[]{:S(2)}) copy-start(f32[3,128,256]{2,1,0:T(8,128)S(1)} %broadcast_multiply_fusion) | copy-start | bytes 1179652

commit v4 on v3

--- a/solution.py
+++ b/solution.py
@@ -19,10 +19,8 @@
 BF16 = jnp.bfloat16
 
 
-(T_WA, T_WAQ, T_W1R, T_W1I, T_W2, T_W2I, T_BR, T_BI, T_W3, T_W3Q, T_S2, T_S2I) = (
-    0, 1, 2, 3, 4, 5, 6, 7, 8, 9, 10, 13,
-)
-N_TABLES = 16
+(T_WA, T_WAQ, T_W1R, T_W1I, T_W2, T_W2I, T_BR, T_BI, T_W3, T_W3Q, T_SF, T_SI) = range(12)
+N_TABLES = 12
 
 
 def angle(left, right, length):
@@ -61,21 +59,23 @@
     ws = np.einsum("ab,id->aidb", eight, sin).reshape(128, 128)
     out[T_W2] = np.block([[wc, -ws], [ws, wc]])
     out[T_W2I] = np.block([[wc.T, ws.T], [-ws.T, wc.T]])
-    for m in range(3):
-        sc, ss = np.zeros((128, 128)), np.zeros((128, 128))
-        for j in range(2):
-            rows = slice(48 * j + 16 * m, 48 * j + 16 * m + 16)
-            cols = slice(16 * j, 16 * j + 16)
-            sc[rows, cols], ss[rows, cols] = cos, sin
-        out[T_S2 + m] = np.block([[sc, -ss], [ss, sc]])
-        out[T_S2I + m] = np.block([[sc.T, ss.T], [-ss.T, sc.T]])
+    four = np.eye(4)
+    sc = np.kron(four, cos)
+    ss = np.kron(four, sin)
+    none = np.zeros((64, 64))
+    out[T_SF, :, :128] = np.block([[sc, -ss], [none, none], [ss, sc], [none, none]])
+    out[T_SI, :128, :128] = np.block([[sc.T, ss.T], [-ss.T, sc.T]])
     return out
 
 
 def two_parts(value):
     high = value.astype(np.float32).astype(ml_dtypes.bfloat16)
     low = (value - high.astype(np.float64)).astype(np.float32).astype(ml_dtypes.bfloat16)
-    return np.stack([high, low])
+    both = np.stack([high, low])
+    for k in (T_SF, T_SI):
+        both[0, k, :, 128:] = low[k, :, :128]
+    both[0, T_SI, 128:, :128] = high[T_SI, :128, :128]
+    return both
 
 
 def twiddles():
@@ -232,9 +232,12 @@
         @pl.when(me == 0)
         def _():
             row_copy().wait_recv()
-            for k in range(4):
-                rows = jnp.concatenate([kr[k], kr2[k], jnp.zeros((96, 256), F32)], 0)
-                kst[k] = rows.T
+            def both(k):
+                return jnp.concatenate([kr[k], kr2[k]], 0)
+
+            kst[0] = jnp.concatenate([both(0), both(1)] * 2, 0).T
+            kst[1] = jnp.concatenate([both(3)] * 4, 0).T
+            kst[2] = jnp.concatenate([both(2)] * 4, 0).T
 
     def step(it, _):
         def place(m, c):
@@ -313,32 +316,40 @@
             kernel_tables()
 
         def mirrored_rows(g, group):
+            dot = functools.partial(jnp.dot, preferred_element_type=F32)
+            halves = lambda v: v[:, :128] + v[:, 128:]
             cos, sin = tw[pl.ds(0, 256), :], tw[pl.ds(256, 256), :]
             seq = jnp.zeros((128, 128), F32)
             for j in range(2):
-                for b, m in enumerate(group):
+                for b in range(len(group)):
                     block = r1[g, pl.ds(2 * j + b, 128, stride=4), :]
-                    at = 48 * j + 16 * m
+                    at = 32 * b + 16 * j
                     inside = jnp.logical_and(lane >= at, lane < at + 16)
                     seq = jnp.where(inside, pltpu.roll(block, at, 1) if at else block, seq)
-            seq = split(seq)
-            ar = product((cb[0, T_W1R][:, :128], cb[1, T_W1R][:, :128]), seq)
-            ai = product((cb[0, T_W1I][:, :128], cb[1, T_W1I][:, :128]), seq)
-            v = split(jnp.concatenate([ar * cos + ai * sin, ai * cos - ar * sin], 1))
-            z = [product(v, table(T_S2 + m)) for m in group]
-            two = lambda k: jnp.concatenate([kst[k], kst[k]], 1)
+            xh, xl = split(seq)
+            x = jnp.concatenate([
+                jnp.concatenate([xh, xl], 1), jnp.concatenate([jnp.zeros_like(xh), xh], 1)], 0)
+            ar, ai = [
+                halves(dot(jnp.concatenate([cb[0, k, :, pl.ds(0, 128)], cb[1, k, :, pl.ds(0, 128)]], 1), x))
+                for k in (T_W1R, T_W1I)
+            ]
+            vh, vl = split(jnp.concatenate([ar * cos + ai * sin, ai * cos - ar * sin], 1))
+            z = halves(dot(vh, cb[0, T_SF])) + dot(vl, cb[0, T_SF, :, pl.ds(0, 128)])
+            wide = lax.broadcasted_iota(jnp.int32, (256, 128), 1)
             if len(group) == 1:
-                field = [two(2) * z[0]]
+                field = kst[2] * z
             else:
-                xx, yy, xy = two(0), two(1), two(3)
-                field = [xx * z[0] + xy * z[1], xy * z[0] + yy * z[1]]
-            back = 0.0
-            for m, f in zip(group, field):
-                back = back + product(split(f), table(T_S2I + m))
-            br, bi = back[:, :128], back[:, 128:]
-            yr, yi = split(br * cos - bi * sin), split(bi * cos + br * sin)
-            os[...] = product((cb[0, T_BR][:128], cb[1, T_BR][:128]), yr) + product(
-                (cb[0, T_BI][:128], cb[1, T_BI][:128]), yi)
+                swapped = jnp.where(lax.rem(wide // 32, 2) == 0, pltpu.roll(z, 96, 1), pltpu.roll(z, 32, 1))
+                field = kst[0] * z + kst[1] * swapped
+            back = halves(dot(jnp.concatenate(split(field), 1), cb[0, T_SI]))
+            turned = pltpu.roll(back, 64, 1) * sin
+            yh, yl = split(back * cos + jnp.where(wide < 64, -turned, turned))
+            y = jnp.concatenate([yh, yl], 1)
+            re, im = [
+                halves(dot(cb[0, k, pl.ds(0, 128), :], y)) + dot(cb[1, k, pl.ds(0, 128), :], yh)
+                for k in (T_BR, T_BI)
+            ]
+            os[...] = re + pltpu.roll(im, 64, 1)
 
         def x_chunk(g, group):
             arrived(g, r1, a_recv)
@@ -383,9 +394,9 @@
             @pl.when(mirrored)
             def _():
                 for j in range(2):
-                    for b, m in enumerate(group):
+                    for b in range(len(group)):
                         rows = pl.ds(2 * j + b, 128, stride=4)
-                        shift = (128 - 48 * j - 16 * m) % 128
+                        shift = (128 - 32 * b - 16 * j) % 128
                         moved = pltpu.roll(os[...], shift, 1) if shift else os[...]
                         s2[g, rows, :] = jnp.where(lane < 16, moved, s2[g, rows, :])
 
@@ -540,7 +551,7 @@
             V((544, 128), F32),
             V(block, F32), V((2,) + band, F32), V(band, F32), V(band, F32), V(band, F32),
             V(band, F32), V((2, 2, 8, 2048), F32), V((4, 2, 256, 128), F32),
-            V((4, 16, 256), F32), V((4, 16, 256), F32), V((4, 256, 128), F32),
+            V((4, 16, 256), F32), V((4, 16, 256), F32), V((3, 256, 128), F32),
             V(slots, F32), V(slots, F32), V(slots, F32), V(slots, F32),
             V((2, 3, 256, 256), BF16), V((2, 256, 256), F32), V((2, 256, 256), BF16), V((2, 2, 256, 256), BF16),
             V((3, 256, 256), F32), V((3, 16, 256), F32), V((128, 128), F32),

time: 76.1 us -> 75.2 us (0.988)
  Pallas kernels: 73.2 us -> 72.3 us
    pallas_call x1, Pallas kernels: 73.2 us -> 72.3 us  [body(): pl.pallas_call(functools.partial(kernel, sizes), out_shape=jax.ShapeDtype...]
where the time goes in v4:
time: 75.2 us; the launch traced here: 75 us
  Pallas kernels  72.3 us (96%)
  other arithmetic  1.98 us (3%)
    pallas_call x1, Pallas kernels, body(): pl.pallas_call(functools.partial(kernel, sizes), out_shape=jax.ShapeDtype...  72.3 us

profile of v4, /device:TPU:1, one launch (start us, length us, event | category | flops | bytes accessed | tf_op | source)
XLA Modules:
  0.0 75.0 jit_solution(4014153828524817384)
XLA Ops:
  0.6 0.0 copy-start
  0.6 0.0 copy-start.2
  0.6 72.3 %shard_map.68 = f32[3,128,256]{2,1,0:T(8,128)} custom-call(f32[3,128,256]{2,1,0:T(8,128)} %mag_h.1, s32[128,256]{1,0:T(8,128)} %occ_h.1, f32[4,32,4096]{2,1,0:T(8,128)} %ks_h.1, bf16[2,12,256,256]{3,2,1,0:T(8,128)(2,1)} %constant.10.clone.cb_h, f32[544,128]{1,0:T(8,128)} %constant.11.clone.tw_h), custom_call_target="tpu_custom_call" | custom-call | tf_op jit(solution)/shard_map/pallas_call | solution.py:544
  73.0 1.0 %broadcast_multiply_fusion = f32[3,128,256]{2,1,0:T(8,128)S(1)} fusion(f32[3,128,256]{2,1,0:T(8,128)} %shard_map.68), kind=kLoop, calls=%fused_computation.1 | loop fusion | flops 98304 | bytes 786432 | tf_op jit(solution)/shard_map/mul | solution.py:567
  74.0 0.0 copy-done
  74.0 0.0 copy-done.2
  74.0 0.0 copy-start.1
  74.0 0.1 divide_bitcast_fusion.2
  74.2 0.1 divide_bitcast_fusion.1
  74.2 0.8 %pad_maximum_fusion = f32[3,128,256]{2,1,0:T(8,128)} fusion(f32[1,128,256]{2,1,0:T(8,128)S(1)} %get-tuple-element.9, f32[1,128,256]{2,1,0:T(8,128)S(1)} %get-tuple-element.8, f32[1,128,256]{2,1,0:T(8,128)S(1)} %get-tuple-element.6), kind=kLoop, calls=%fused_computation | loop fusion | flops 196608 | bytes 786432 | tf_op jit(solution)/shard_map/stack | solution.py:570
  75.0 0.0 copy-done.1
Async XLA Ops:
  0.6 73.4 %copy-start = (f32[3,128,256]{2,1,0:T(8,128)S(1)}, f32[3,128,256]{2,1,0:T(8,128)}, u32[]{:S(2)}) copy-start(f32[3,128,256]{2,1,0:T(8,128)} %mag_h.1) | copy-start | bytes 1179652
  0.6 73.4 %copy-start.2 = (s32[128,256]{1,0:T(8,128)S(1)}, s32[128,256]{1,0:T(8,128)}, u32[]{:S(2)}) copy-start(s32[128,256]{1,0:T(8,128)} %occ_h.1) | copy-start | bytes 393220
  74.0 1.0 %copy-start.1 = (f32[3,128,256]{2,1,0:T(8,128)}, f32[3,128,256]{2,1,0:T(8,128)S(1)}, u32[]{:S(2)}) copy-start(f32[3,128,256]{2,1,0:T(8,128)S(1)} %broadcast_multiply_fusion) | copy-start | bytes 1179652

commit v5 on v4

--- a/solution.py
+++ b/solution.py
@@ -119,7 +119,7 @@
 
 
 def kernel(sizes, mag_h, occ_h, ks_h, cb_h, tw_h, out_ref, mag, occ, ks, cb, tw, m0l, fb, k1, dm, ex,
-           mr, hb, kt, kr, kr2, kst, s1, r1, s2, r2, u, zb, xs, ys, pb, pq, os, load_sem, ty_send, ty_recv,
+           mr, hb, kt, kr, kr2, kst, s1, r1, s2, r2, u, zb, xs, ys, pb, pq, load_sem, ty_send, ty_recv,
            h_send, h_recv, k_send, k_recv, a_send, a_recv, b_send, b_recv, f_send, f_recv, ready):
     n_x, n_y, n_z = sizes
     n_ty = 2 * n_z
@@ -333,8 +333,10 @@
                 halves(dot(jnp.concatenate([cb[0, k, :, pl.ds(0, 128)], cb[1, k, :, pl.ds(0, 128)]], 1), x))
                 for k in (T_W1R, T_W1I)
             ]
+            yield None
             vh, vl = split(jnp.concatenate([ar * cos + ai * sin, ai * cos - ar * sin], 1))
             z = halves(dot(vh, cb[0, T_SF])) + dot(vl, cb[0, T_SF, :, pl.ds(0, 128)])
+            yield None
             wide = lax.broadcasted_iota(jnp.int32, (256, 128), 1)
             if len(group) == 1:
                 field = kst[2] * z
@@ -342,6 +344,7 @@
                 swapped = jnp.where(lax.rem(wide // 32, 2) == 0, pltpu.roll(z, 96, 1), pltpu.roll(z, 32, 1))
                 field = kst[0] * z + kst[1] * swapped
             back = halves(dot(jnp.concatenate(split(field), 1), cb[0, T_SI]))
+            yield None
             turned = pltpu.roll(back, 64, 1) * sin
             yh, yl = split(back * cos + jnp.where(wide < 64, -turned, turned))
             y = jnp.concatenate([yh, yl], 1)
@@ -349,10 +352,10 @@
                 halves(dot(cb[0, k, pl.ds(0, 128), :], y)) + dot(cb[1, k, pl.ds(0, 128), :], yh)
                 for k in (T_BR, T_BI)
             ]
-            os[...] = re + pltpu.roll(im, 64, 1)
-
-        def x_chunk(g, group):
-            arrived(g, r1, a_recv)
+            yield re + pltpu.roll(im, 64, 1)
+
+        def x_core(g, group, mirrored):
+            aside = mirrored_rows(g, group) if mirrored else iter([None] * 4)
             for part in range(2):
                 for b in range(2):
                     block = r1[g, pl.ds(2 * part + b, 128, stride=4), :]
@@ -360,18 +363,14 @@
                         xs[k, pl.ds(128 * part, 128), pl.ds(128 * b, 128)] = piece
             x = (xs[0], xs[1])
             tr, ti = product(table(T_W1R), x), product(table(T_W1I), x)
+            next(aside)
             cos, sin = tw[pl.ds(0, 256), :], tw[pl.ds(256, 256), :]
             for b in range(2):
                 ar, ai = tr[:, 128 * b:128 * b + 128], ti[:, 128 * b:128 * b + 128]
                 v = jnp.concatenate([ar * cos + ai * sin, ai * cos - ar * sin], 1)
                 zb[b] = product(split(v), table(T_W2))
 
-            mirrored = me == 0 if len(group) == 1 else jnp.logical_and(me == 0, g == 1)
-
-            @pl.when(mirrored)
-            def _():
-                mirrored_rows(g, group)
-
+            next(aside)
             for b in range(2):
                 pieces = []
                 for part in range(2):
@@ -381,25 +380,33 @@
                     else:
                         pieces.append(kt[b, g - 1] * zb[b, :, cols] + kt[3, g - 1] * zb[1 - b, :, cols])
                 p = product(split(jnp.concatenate(pieces, 1)), table(T_W2I))
+                if b == 0:
+                    next(aside)
                 pr, pi = p[:, :128], p[:, 128:]
                 for part, v in enumerate((pr * cos - pi * sin, pi * cos + pr * sin)):
                     for k, piece in enumerate(split(v)):
                         ys[k, part, :, pl.ds(128 * b, 128)] = piece
+            moved = next(aside)
             o = product(table(T_BR), (ys[0, 0], ys[1, 0])) + product(table(T_BI), (ys[0, 1], ys[1, 1]))
             for part in range(2):
                 for b in range(2):
                     s2[g, pl.ds(2 * part + b, 128, stride=4), :] = (
                         o[128 * part:128 * part + 128, 128 * b:128 * b + 128])
 
-            @pl.when(mirrored)
-            def _():
+            if mirrored:
                 for j in range(2):
                     for b in range(len(group)):
                         rows = pl.ds(2 * j + b, 128, stride=4)
                         shift = (128 - 32 * b - 16 * j) % 128
-                        moved = pltpu.roll(os[...], shift, 1) if shift else os[...]
-                        s2[g, rows, :] = jnp.where(lane < 16, moved, s2[g, rows, :])
-
+                        own_lanes = pltpu.roll(moved, shift, 1) if shift else moved
+                        block = o[128 * j:128 * j + 128, 128 * b:128 * b + 128]
+                        s2[g, rows, :] = jnp.where(lane < 16, own_lanes, block)
+
+        def x_chunk(g, group):
+            arrived(g, r1, a_recv)
+            mirrored = me == 0 if len(group) == 1 else jnp.logical_and(me == 0, g == 1)
+            pl.when(mirrored)(lambda: x_core(g, group, True))
+            pl.when(jnp.logical_not(mirrored))(lambda: x_core(g, group, False))
             exchange(g, s2, r2, b_send, b_recv)
 
         def xy_chunk(g, _):
@@ -554,7 +561,7 @@
             V((4, 16, 256), F32), V((4, 16, 256), F32), V((3, 256, 128), F32),
             V(slots, F32), V(slots, F32), V(slots, F32), V(slots, F32),
             V((2, 3, 256, 256), BF16), V((2, 256, 256), F32), V((2, 256, 256), BF16), V((2, 2, 256, 256), BF16),
-            V((3, 256, 256), F32), V((3, 16, 256), F32), V((128, 128), F32),
+            V((3, 256, 256), F32), V((3, 16, 256), F32),
             D((5,)), D, D((3,)), D((2,)), D((2, 2)), D, D, D, D((3,)), D, D((3,)), D, D,
             pltpu.SemaphoreType.REGULAR,
         ],

time: 75.2 us -> 73.6 us (0.979)
  Pallas kernels: 72.3 us -> 70.8 us
    pallas_call x1, Pallas kernels: 72.3 us -> 70.8 us  [body(): pl.pallas_call(functools.partial(kernel, sizes), out_shape=jax.ShapeDtype...]
where the time goes in v5:
time: 73.6 us; the launch traced here: 73.5 us
  Pallas kernels  70.8 us (96%)
  other arithmetic  1.98 us (3%)
    pallas_call x1, Pallas kernels, body(): pl.pallas_call(functools.partial(kernel, sizes), out_shape=jax.ShapeDtype...  70.8 us

profile of v5, /device:TPU:1, one launch (start us, length us, event | category | flops | bytes accessed | tf_op | source)
XLA Modules:
  0.0 73.5 jit_solution(3423030593915560682)
XLA Ops:
  0.6 0.0 copy-start
  0.6 0.0 copy-start.2
  0.6 70.8 %shard_map.68 = f32[3,128,256]{2,1,0:T(8,128)} custom-call(f32[3,128,256]{2,1,0:T(8,128)} %mag_h.1, s32[128,256]{1,0:T(8,128)} %occ_h.1, f32[4,32,4096]{2,1,0:T(8,128)} %ks_h.1, bf16[2,12,256,256]{3,2,1,0:T(8,128)(2,1)} %constant.10.clone.cb_h, f32[544,128]{1,0:T(8,128)} %constant.11.clone.tw_h), custom_call_target="tpu_custom_call" | custom-call | tf_op jit(solution)/shard_map/pallas_call | solution.py:551
  71.5 1.0 %broadcast_multiply_fusion = f32[3,128,256]{2,1,0:T(8,128)S(1)} fusion(f32[3,128,256]{2,1,0:T(8,128)} %shard_map.68), kind=kLoop, calls=%fused_computation.1 | loop fusion | flops 98304 | bytes 786432 | tf_op jit(solution)/shard_map/mul | solution.py:574
  72.5 0.0 copy-done
  72.5 0.0 copy-done.2
  72.5 0.0 copy-start.1
  72.5 0.1 divide_bitcast_fusion.2
  72.6 0.1 divide_bitcast_fusion.1
  72.7 0.8 %pad_maximum_fusion = f32[3,128,256]{2,1,0:T(8,128)} fusion(f32[1,128,256]{2,1,0:T(8,128)S(1)} %get-tuple-element.9, f32[1,128,256]{2,1,0:T(8,128)S(1)} %get-tuple-element.8, f32[1,128,256]{2,1,0:T(8,128)S(1)} %get-tuple-element.6), kind=kLoop, calls=%fused_computation | loop fusion | flops 196608 | bytes 786432 | tf_op jit(solution)/shard_map/stack | solution.py:577
  73.5 0.0 copy-done.1
Async XLA Ops:
  0.6 71.9 %copy-start = (f32[3,128,256]{2,1,0:T(8,128)S(1)}, f32[3,128,256]{2,1,0:T(8,128)}, u32[]{:S(2)}) copy-start(f32[3,128,256]{2,1,0:T(8,128)} %mag_h.1) | copy-start | bytes 1179652
  0.6 71.9 %copy-start.2 = (s32[128,256]{1,0:T(8,128)S(1)}, s32[128,256]{1,0:T(8,128)}, u32[]{:S(2)}) copy-start(s32[128,256]{1,0:T(8,128)} %occ_h.1) | copy-start | bytes 393220
  72.5 1.0 %copy-start.1 = (f32[3,128,256]{2,1,0:T(8,128)}, f32[3,128,256]{2,1,0:T(8,128)S(1)}, u32[]{:S(2)}) copy-start(f32[3,128,256]{2,1,0:T(8,128)S(1)} %broadcast_multiply_fusion) | copy-start | bytes 1179652

commit v6 on v5

--- a/solution.py
+++ b/solution.py
@@ -119,7 +119,7 @@
 
 
 def kernel(sizes, mag_h, occ_h, ks_h, cb_h, tw_h, out_ref, mag, occ, ks, cb, tw, m0l, fb, k1, dm, ex,
-           mr, hb, kt, kr, kr2, kst, s1, r1, s2, r2, u, zb, xs, ys, pb, pq, load_sem, ty_send, ty_recv,
+           mr, hb, kt, kr, kr2, kst, s1, r1, s2, r2, u, xs, ys, pb, pq, load_sem, ty_send, ty_recv,
            h_send, h_recv, k_send, k_recv, a_send, a_recv, b_send, b_recv, f_send, f_recv, ready):
     n_x, n_y, n_z = sizes
     n_ty = 2 * n_z
@@ -133,6 +133,13 @@
     at_c = [pc, 1 - pc]
     others = far_first(n_x, n_y, n_z)
 
+    barrier = pltpu.get_barrier_semaphore()
+    line = [o for o in others if o[:2] == (0, 0)]
+    plane = [o for o in others if o[2:] == (0, 0)]
+    for dx, dy, dz, dc in plane + line:
+        to = (at_x[dx] + at_y[dy], at_z[dz] + at_c[dc])
+        pl.semaphore_signal(barrier, inc=1, device_id=to, device_id_type=MESH)
+
     loads = [
         pltpu.make_async_copy(mag_h, mag, load_sem.at[0]),
         pltpu.make_async_copy(occ_h, occ, load_sem.at[1]),
@@ -142,13 +149,6 @@
     ]
     for k in (0, 1, 4, 3, 2):
         loads[k].start()
-
-    barrier = pltpu.get_barrier_semaphore()
-    line = [o for o in others if o[:2] == (0, 0)]
-    plane = [o for o in others if o[2:] == (0, 0)]
-    for dx, dy, dz, dc in plane + line:
-        to = (at_x[dx] + at_y[dy], at_z[dz] + at_c[dc])
-        pl.semaphore_signal(barrier, inc=1, device_id=to, device_id_type=MESH)
     loads[0].wait()
     loads[1].wait()
     occf = occ[...].astype(F32)
@@ -243,7 +243,8 @@
         def place(m, c):
             if isinstance(m, int) and m == 2:
                 return 0, 16 * c
-            return 1 + c // 8, pl.multiple_of(128 * m + 16 * (c % 8), 16)
+            start = 128 * m + 16 * (c % 8)
+            return 1 + c // 8, start if isinstance(m, int) else pl.multiple_of(start, 16)
 
         def y_first(m, _):
             @pl.when(it == 0)
@@ -356,29 +357,27 @@
 
         def x_core(g, group, mirrored):
             aside = mirrored_rows(g, group) if mirrored else iter([None] * 4)
-            for part in range(2):
-                for b in range(2):
-                    block = r1[g, pl.ds(2 * part + b, 128, stride=4), :]
-                    for k, piece in enumerate(split(block)):
-                        xs[k, pl.ds(128 * part, 128), pl.ds(128 * b, 128)] = piece
-            x = (xs[0], xs[1])
+            x = split(jnp.concatenate([
+                jnp.concatenate([r1[g, pl.ds(2 * part + b, 128, stride=4), :] for b in range(2)], 1)
+                for part in range(2)], 0))
             tr, ti = product(table(T_W1R), x), product(table(T_W1I), x)
             next(aside)
             cos, sin = tw[pl.ds(0, 256), :], tw[pl.ds(256, 256), :]
+            zs = []
             for b in range(2):
                 ar, ai = tr[:, 128 * b:128 * b + 128], ti[:, 128 * b:128 * b + 128]
                 v = jnp.concatenate([ar * cos + ai * sin, ai * cos - ar * sin], 1)
-                zb[b] = product(split(v), table(T_W2))
+                zs.append(product(split(v), table(T_W2)))
 
             next(aside)
             for b in range(2):
                 pieces = []
                 for part in range(2):
-                    cols = pl.ds(128 * part, 128)
+                    cols = slice(128 * part, 128 * part + 128)
                     if len(group) == 1:
-                        pieces.append(kt[2, b] * zb[b, :, cols])
+                        pieces.append(kt[2, b] * zs[b][:, cols])
                     else:
-                        pieces.append(kt[b, g - 1] * zb[b, :, cols] + kt[3, g - 1] * zb[1 - b, :, cols])
+                        pieces.append(kt[b, g - 1] * zs[b][:, cols] + kt[3, g - 1] * zs[1 - b][:, cols])
                 p = product(split(jnp.concatenate(pieces, 1)), table(T_W2I))
                 if b == 0:
                     next(aside)
@@ -436,14 +435,15 @@
             arrived(g, r2, b_recv)
             for part in range(2):
                 for b in range(2):
-                    block = r2[g, pl.ds(2 * part + b, 128, stride=4), :].T
+                    block = r2[g, pl.ds(2 * part + b, 128, stride=4), :]
                     for k, piece in enumerate(split(block)):
-                        xs[k, pl.ds(128 * b, 128), pl.ds(128 * part, 128)] = piece
-            pb[g] = product((xs[0], xs[1]), table(T_W3))
+                        xs[k, pl.ds(128 * part, 128), pl.ds(128 * b, 128)] = piece
+            rows_first = (((0,), (0,)), ((), ()))
+            pb[g] = product((xs[0], xs[1]), table(T_W3), rows_first)
 
             def ends(m, row):
-                rows = pl.ds(row, 16)
-                pq[m] = product((xs[0, rows, :], xs[1, rows, :]), table(T_W3Q))
+                cols = pl.ds(row, 128)
+                pq[m] = product((xs[0, :, cols], xs[1, :, cols]), table(T_W3Q), rows_first)[:16]
 
             if isinstance(g, int):
                 ends(2, 0)
@@ -486,7 +486,8 @@
         y_inverse_first(0, 0)
         y_inverse_second(2, 0)
         lax.fori_loop(1, 3, y_inverse_first, 0)
-        lax.fori_loop(0, 2, y_inverse_second, 0)
+        y_inverse_second(0, 0)
+        y_inverse_second(1, 0)
 
         def advance(j, _):
             far = j // 2
@@ -560,7 +561,7 @@
             V(band, F32), V((2, 2, 8, 2048), F32), V((4, 2, 256, 128), F32),
             V((4, 16, 256), F32), V((4, 16, 256), F32), V((3, 256, 128), F32),
             V(slots, F32), V(slots, F32), V(slots, F32), V(slots, F32),
-            V((2, 3, 256, 256), BF16), V((2, 256, 256), F32), V((2, 256, 256), BF16), V((2, 2, 256, 256), BF16),
+            V((2, 3, 256, 256), BF16), V((2, 256, 256), BF16), V((2, 2, 256, 256), BF16),
             V((3, 256, 256), F32), V((3, 16, 256), F32),
             D((5,)), D, D((3,)), D((2,)), D((2, 2)), D, D, D, D((3,)), D, D((3,)), D, D,
             pltpu.SemaphoreType.REGULAR,

time: 73.6 us -> 73.6 us (level)
  no operation moved by 1% of the time
where the time goes in v6:
time: 73.6 us; the launch traced here: 73.5 us
  Pallas kernels  70.8 us (96%)
  other arithmetic  1.98 us (3%)
    pallas_call x1, Pallas kernels, body(): pl.pallas_call(functools.partial(kernel, sizes), out_shape=jax.ShapeDtype...  70.8 us

profile of v6, /device:TPU:1, one launch (start us, length us, event | category | flops | bytes accessed | tf_op | source)
XLA Modules:
  0.0 73.5 jit_solution(8370154950613392517)
XLA Ops:
  0.6 0.0 copy-start
  0.6 0.0 copy-start.2
  0.6 70.8 %shard_map.68 = f32[3,128,256]{2,1,0:T(8,128)} custom-call(f32[3,128,256]{2,1,0:T(8,128)} %mag_h.1, s32[128,256]{1,0:T(8,128)} %occ_h.1, f32[4,32,4096]{2,1,0:T(8,128)} %ks_h.1, bf16[2,12,256,256]{3,2,1,0:T(8,128)(2,1)} %constant.10.clone.cb_h, f32[544,128]{1,0:T(8,128)} %constant.11.clone.tw_h), custom_call_target="tpu_custom_call" | custom-call | tf_op jit(solution)/shard_map/pallas_call | solution.py:552
  71.4 1.0 %broadcast_multiply_fusion = f32[3,128,256]{2,1,0:T(8,128)S(1)} fusion(f32[3,128,256]{2,1,0:T(8,128)} %shard_map.68), kind=kLoop, calls=%fused_computation.1 | loop fusion | flops 98304 | bytes 786432 | tf_op jit(solution)/shard_map/mul | solution.py:575
  72.4 0.0 copy-done
  72.5 0.0 copy-done.2
  72.5 0.0 copy-start.1
  72.5 0.1 divide_bitcast_fusion.2
  72.6 0.1 divide_bitcast_fusion.1
  72.7 0.8 %pad_maximum_fusion = f32[3,128,256]{2,1,0:T(8,128)} fusion(f32[1,128,256]{2,1,0:T(8,128)S(1)} %get-tuple-element.9, f32[1,128,256]{2,1,0:T(8,128)S(1)} %get-tuple-element.8, f32[1,128,256]{2,1,0:T(8,128)S(1)} %get-tuple-element.6), kind=kLoop, calls=%fused_computation | loop fusion | flops 196608 | bytes 786432 | tf_op jit(solution)/shard_map/stack | solution.py:578
  73.5 0.0 copy-done.1
Async XLA Ops:
  0.6 71.8 %copy-start = (f32[3,128,256]{2,1,0:T(8,128)S(1)}, f32[3,128,256]{2,1,0:T(8,128)}, u32[]{:S(2)}) copy-start(f32[3,128,256]{2,1,0:T(8,128)} %mag_h.1) | copy-start | bytes 1179652
  0.6 71.8 %copy-start.2 = (s32[128,256]{1,0:T(8,128)S(1)}, s32[128,256]{1,0:T(8,128)}, u32[]{:S(2)}) copy-start(s32[128,256]{1,0:T(8,128)} %occ_h.1) | copy-start | bytes 393220
  72.5 1.0 %copy-start.1 = (f32[3,128,256]{2,1,0:T(8,128)}, f32[3,128,256]{2,1,0:T(8,128)S(1)}, u32[]{:S(2)}) copy-start(f32[3,128,256]{2,1,0:T(8,128)S(1)} %broadcast_multiply_fusion) | copy-start | bytes 1179652
